TPU v7x, 256 devices: a whole 4x4x8 slice. The times are simulated.
256 devices in a mesh: outer: 32 (over z, x), inner: 8 (over y, core).
Axes of the slice: x: 4, y: 4, z: 8, core: 2. Of those that a mesh axis runs over, the one named last changes fastest.
Arguments:
- queries: bfloat16 [32768, 2048], P(('outer', 'inner')), may hold values from -5 to 5
- key_rows: bfloat16 [32768, 2048], P(('outer', 'inner')), may hold values from -5 to 5
- value_rows: bfloat16 [32768, 2048], P(('outer', 'inner')), may hold values from -6 to 6
- out_grad: bfloat16 [32768, 2048], P(('outer', 'inner')), may hold values from -6 to 6
- log_gate: float32 [16, 32768], P(None, ('outer', 'inner')), may hold values from -1 to 0
Outputs:
- mixed_out: bfloat16 [32768, 2048], P(('outer', 'inner'))
- query_grad: bfloat16 [32768, 2048], P(('outer', 'inner'))
- key_grad: bfloat16 [32768, 2048], P(('outer', 'inner'))
- value_grad: bfloat16 [32768, 2048], P(('outer', 'inner'))
All inputs are finite; a program needn't handle non-finite values.
Results may differ from a plain program's by a relative error of at most 0.007.
Values may be sent and summed in bfloat16 or wider, within the bound.
No kernel may reach another device: no remote copies, remote signals or barrier semaphores. Data moves between devices by JAX's collectives and lax.ppermute only.
A program may use at most 256 MiB of HBM per device.

v0:
```python
import jax
import jax.numpy as jnp
from jax import lax
from jax.sharding import PartitionSpec as P

W = 64


def from_behind(value, axis, steps):
    count = lax.axis_size(axis)
    first, last = (max(0, -steps), min(count, count - steps))
    return lax.ppermute(value, axis, [(source, source + steps) for source in range(first, last)])


def carried_in(part, axis, combine, identity, reverse):
    count = lax.axis_size(axis)
    place = lax.axis_index(axis)
    ahead = count - 1 - place if reverse else place
    gathered = jax.tree.map(lambda a: lax.all_gather(a, axis), part)
    state = jax.tree.map(lambda a, e: jnp.zeros_like(a) + jnp.asarray(e, a.dtype), part, identity)

    def one(hop, state):
        source = count - 1 - hop if reverse else hop
        return combine(
            state, jax.tree.map(lambda a: lax.dynamic_index_in_dim(a, source, 0, False), gathered)
        )

    return lax.fori_loop(0, ahead, one, state)


def low_product(form, left, right):
    return jnp.einsum(form, left, right, preferred_element_type=jnp.float32)


def high_product(form, left, right):
    return jnp.einsum(form, left, right, precision=lax.Precision.HIGHEST)


def local_states(query_blk, key_blk, value_blk, grad_blk, gate_rows):
    cumul_gate = jnp.cumsum(gate_rows, axis=1)
    last_cumul = cumul_gate[:, -1:]
    block_decay = jnp.exp(cumul_gate[:, -1])
    tail_weight = jnp.exp(last_cumul - cumul_gate).T
    head_weight = jnp.exp(cumul_gate).T
    state_local = high_product(
        "thf,the->hfe",
        key_blk.astype(jnp.float32) * tail_weight[:, :, None],
        value_blk.astype(jnp.float32),
    )
    grad_local = high_product(
        "thf,the->hfe",
        query_blk.astype(jnp.float32) * head_weight[:, :, None],
        grad_blk.astype(jnp.float32),
    )
    return (block_decay, state_local, grad_local)


def block_terms(
    query_blk,
    key_blk,
    value_blk,
    grad_blk,
    gate_rows,
    state_in,
    grad_after,
    key_halo,
    value_halo,
    halo_live,
    lin_scale,
):
    row_count = query_blk.shape[0]
    halo_rows = key_halo.shape[0]
    head_size = query_blk.shape[2]
    cumul_gate = jnp.cumsum(gate_rows, axis=1)
    last_cumul = cumul_gate[:, -1:]
    head_weight = jnp.exp(cumul_gate).T
    tail_weight = jnp.exp(last_cumul - cumul_gate).T
    query_pos = jnp.arange(row_count)[:, None]
    key_pos = jnp.arange(row_count)[None, :]
    causal_mask = (key_pos <= query_pos)[None]
    gap_logs = cumul_gate[:, :, None] - cumul_gate[:, None, :]
    decay_grid = jnp.where(causal_mask, jnp.exp(jnp.where(causal_mask, gap_logs, 0.0)), 0.0)
    lin_weight = (low_product("thf,shf->hts", query_blk, key_blk) * decay_grid).astype(jnp.bfloat16)
    query_decayed = query_blk.astype(jnp.float32) * head_weight[:, :, None]
    lin_out = low_product("hts,she->the", lin_weight, value_blk) + high_product(
        "thf,hfe->the", query_decayed, state_in
    )
    ext_keys = jnp.concatenate([key_halo, key_blk], axis=0)
    ext_values = jnp.concatenate([value_halo, value_blk], axis=0)
    ext_pos = jnp.arange(row_count + halo_rows)[None, :]
    in_band = (
        (ext_pos > query_pos)
        & (ext_pos <= query_pos + halo_rows)
        & ((ext_pos >= halo_rows) | halo_live)
    )[None]
    logits = low_product("thf,jhf->htj", query_blk, ext_keys) * head_size ** (-0.5)
    masked_logits = jnp.where(in_band, logits, -jnp.inf)
    row_max = jnp.max(masked_logits, axis=2, keepdims=True)
    expo_terms = jnp.exp(masked_logits - row_max)
    win_prob = expo_terms / jnp.sum(expo_terms, axis=2, keepdims=True)
    prob_low = win_prob.astype(jnp.bfloat16)
    win_out = low_product("htj,jhe->the", prob_low, ext_values)
    output = (lin_scale * lin_out + win_out).astype(jnp.bfloat16)
    grad_weight = (low_product("the,she->hts", grad_blk, value_blk) * decay_grid).astype(
        jnp.bfloat16
    )
    grad_decayed = grad_blk.astype(jnp.float32) * head_weight[:, :, None]
    query_lin = low_product("hts,shf->thf", grad_weight, key_blk) + high_product(
        "the,hfe->thf", grad_decayed, state_in
    )
    value_tail = value_blk.astype(jnp.float32) * tail_weight[:, :, None]
    key_tail = key_blk.astype(jnp.float32) * tail_weight[:, :, None]
    key_lin = low_product("hts,thf->shf", grad_weight, query_blk) + high_product(
        "she,hfe->shf", value_tail, grad_after
    )
    value_lin = low_product("hts,the->she", lin_weight, grad_blk) + high_product(
        "shf,hfe->she", key_tail, grad_after
    )
    prob_grad = low_product("the,jhe->htj", grad_blk, ext_values)
    row_delta = jnp.sum(win_prob * prob_grad, axis=2, keepdims=True)
    logit_grad = (win_prob * (prob_grad - row_delta) * head_size ** (-0.5)).astype(jnp.bfloat16)
    query_win = low_product("htj,jhf->thf", logit_grad, ext_keys)
    key_ext = low_product("htj,thf->jhf", logit_grad, query_blk)
    value_ext = low_product("htj,the->jhe", prob_low, grad_blk)
    query_grad = (lin_scale * query_lin + query_win).astype(jnp.bfloat16)
    key_local = lin_scale * key_lin + key_ext[halo_rows:]
    value_local = lin_scale * value_lin + value_ext[halo_rows:]
    return (output, query_grad, key_local, value_local, key_ext[:halo_rows], value_ext[:halo_rows])


def forward_merge(earlier_part, later_part):
    return (
        earlier_part[0] * later_part[0],
        later_part[0][:, None, None] * earlier_part[1] + later_part[1],
    )


def backward_merge(earlier_part, later_part):
    return (
        earlier_part[0] * later_part[0],
        later_part[1] + later_part[0][:, None, None] * earlier_part[1],
    )


def run_forward(running, element):
    return (forward_merge(running, element), running)


def run_backward(running, element):
    return (backward_merge(running, element), running)


def select_mine(bundle, inner_pos):
    return tuple(
        (lax.dynamic_index_in_dim(member, inner_pos, 0, keepdims=False) for member in bundle)
    )


def per_device(queries, key_rows, value_rows, out_grad, log_gate):
    row_count = queries.shape[0]
    head_count = log_gate.shape[0]
    head_size = queries.shape[1] // head_count
    devices = lax.axis_size("outer") * lax.axis_size("inner")
    lin_scale = (head_size * row_count * devices) ** (-0.5)
    block_shape = (row_count, head_count, head_size)
    query_blk = queries.reshape(block_shape)
    key_blk = key_rows.reshape(block_shape)
    value_blk = value_rows.reshape(block_shape)
    grad_blk = out_grad.reshape(block_shape)
    block_decay, state_local, grad_local = local_states(
        query_blk, key_blk, value_blk, grad_blk, log_gate
    )
    key_halo, value_halo = from_behind((key_blk[-W:], value_blk[-W:]), ("outer", "inner"), 1)
    position = lax.axis_index("outer") * lax.axis_size("inner") + lax.axis_index("inner")
    identity_pair = (
        jnp.ones((head_count,), jnp.float32),
        jnp.zeros((head_count, head_size, head_size), jnp.float32),
    )
    gathered = (
        lax.all_gather(block_decay[None], "inner", axis=0, tiled=True),
        lax.all_gather(state_local[None], "inner", axis=0, tiled=True),
        lax.all_gather(grad_local[None], "inner", axis=0, tiled=True),
    )
    group_decay, group_state, group_grad = gathered
    total_forward, before_forward = lax.scan(run_forward, identity_pair, (group_decay, group_state))
    total_backward, after_backward = lax.scan(
        run_backward, identity_pair, (group_decay, group_grad), reverse=True
    )
    inner_pos = lax.axis_index("inner")
    mine_forward = select_mine(before_forward, inner_pos)
    mine_backward = select_mine(after_backward, inner_pos)
    outer_forward = carried_in(total_forward, "outer", forward_merge, identity_pair, False)
    outer_backward = carried_in(total_backward, "outer", backward_merge, identity_pair, True)
    forward_pair = forward_merge(outer_forward, mine_forward)
    backward_pair = backward_merge(outer_backward, mine_backward)
    output, query_grad, key_local, value_local, key_back, value_back = block_terms(
        query_blk,
        key_blk,
        value_blk,
        grad_blk,
        log_gate,
        forward_pair[1],
        backward_pair[1],
        key_halo,
        value_halo,
        position > 0,
        lin_scale,
    )
    key_return, value_return = (
        from_behind(key_back.astype(jnp.bfloat16), ("outer", "inner"), -1).astype(key_back.dtype),
        from_behind(value_back.astype(jnp.bfloat16), ("outer", "inner"), -1).astype(
            value_back.dtype
        ),
    )
    key_grad = key_local.at[-W:].add(key_return).astype(jnp.bfloat16)
    value_grad = value_local.at[-W:].add(value_return).astype(jnp.bfloat16)
    flat_shape = (row_count, head_count * head_size)
    return (
        output.reshape(flat_shape),
        query_grad.reshape(flat_shape),
        key_grad.reshape(flat_shape),
        value_grad.reshape(flat_shape),
    )


def solution(mesh):
    placed = (
        P(("outer", "inner"), None),
        P(("outer", "inner"), None),
        P(("outer", "inner"), None),
        P(("outer", "inner"), None),
        P(None, ("outer", "inner")),
    )
    return jax.shard_map(
        per_device,
        mesh=mesh,
        in_specs=placed,
        out_specs=(
            P(("outer", "inner"), None),
            P(("outer", "inner"), None),
            P(("outer", "inner"), None),
            P(("outer", "inner"), None),
        ),
        check_vma=False,
    )
```

profile of v0, /device:TPU:230, one launch (start us, length us, event | category | flops | bytes accessed | tf_op | source)
XLA Modules:
  0.0 660.7 jit_solution(8102679605573216670)
XLA Ops:
  18.4 15.5 %all-reduce = f32[128]{0:T(128)S(1)} all-reduce(f32[128]{0:T(128)S(1)} %dynamic-update-slice.6), channel_id=2, replica_groups=mesh['outer'=32,'inner'=8] {'inner'}, use_global_device_ids=true, to_apply=%add | all-reduce | flops 128 | bytes 1024
  34.0 32.2 %all-gather.16.cloned.1.call-done = f32[128,128,128]{2,1,0:T(8,128)} async-done(((f32[16,128,128]{2,1,0:T(8,128)}), f32[128,128,128]{2,1,0:T(8,128)}) %all-gather.16.cloned.1.call-update) | async-done | bytes 8388624 | tf_op jit(solution)/shard_map/all_gather | solution.py:182
  66.1 4.4 broadcast.104.clone.1
  70.5 21.0 %while.69 = (s32[]{:T(128)}, f32[16]{0:T(128)S(1)}, f32[16,128,128]{2,1,0:T(8,128)S(1)}, f32[8,16]{1,0:T(8,128)S(1)}, f32[8,16,128,128]{3,2,1,0:T(8,128)}, /*ind...) while((s32[]{:T(128)}, f32[16]{0:T(128)S(1)}, ...), condition=%wide.region_9.10_spmd.clone, body=%wide.region_8.9_spmd.clone.sunk | while | flops 1048612 | bytes 5243533 | solution.py:186
  92.6 27.8 %all-gather.12.cloned.1.call-done = f32[128,128,128]{2,1,0:T(8,128)} async-done(((f32[16,128,128]{2,1,0:T(8,128)}), f32[128,128,128]{2,1,0:T(8,128)}) %all-gather.12.cloned.1.call-update) | async-done | bytes 8388624 | tf_op jit(solution)/shard_map/all_gather | solution.py:181
  120.4 4.3 broadcast.104.clone
  124.7 20.6 %while.68 = (s32[]{:T(128)}, f32[16]{0:T(128)S(1)}, f32[16,128,128]{2,1,0:T(8,128)S(1)}, f32[8,16]{1,0:T(8,128)S(1)}, f32[8,16,128,128]{3,2,1,0:T(8,128)}, /*ind...) while((s32[]{:T(128)}, f32[16]{0:T(128)S(1)}, ...), condition=%wide.region_2.3_spmd.clone, body=%wide.region_1.2_spmd.clone.sunk | while | flops 1048611 | bytes 5244021 | solution.py:185
  151.2 2.5 collective-permute-start
  160.0 2.6 collective-permute-done.1
  162.6 2.7 fusion.70
  165.3 3.3 convolution_bitcast_fusion
  170.8 2.5 collective-permute-start.3
  175.8 4.8 convolution_bitcast_fusion.1
  185.4 72.2 %all-reduce.3 = (f32[512]{0:T(512)S(1)}, f32[512]{0:T(512)S(1)}) all-reduce(f32[512]{0:T(512)S(1)} %dynamic-update-slice.7, f32[512]{0:T(512)S(1)} %dynamic-update-slice.8), channel_id=4, replica_groups=mesh['outer'=32,'inner'=8] {'outer'}, use_global_device_ids=true, to_apply=%add.1 | all-reduce | flops 1024 | bytes 8192
  257.7 100.4 %all-gather.18.cloned.1.call-done = f32[512,128,128]{2,1,0:T(8,128)} async-done(((f32[16,128,128]{2,1,0:T(8,128)}), f32[512,128,128]{2,1,0:T(8,128)}) %all-gather.18.cloned.1.call-update) | async-done | bytes 33554448 | tf_op jit(solution)/shard_map/all_gather | solution.py:19
  358.5 3.3 convolution_bitcast_fusion.4
  365.6 7.0 %scatter-add.9 = f32[128,16,128]{0,2,1:T(8,128)} dynamic-update-slice(f32[128,16,128]{0,2,1:T(8,128)} %copy-done.2, f32[64,16,128]{0,2,1:T(8,128)} %slice_add_fusion, s32[]{:T(128)} %constant.187.clone.1, s32[]{:T(128)} %constant.180.clone.1, s32[]{:T(128)} %constant.180.clone.1) | dynamic-update-slice | bytes 1048580 | tf_op jit(solution)/shard_map/scatter-add | solution.py:216
  375.1 2.8 convolution_bitcast_fusion.5
  379.7 5.1 scatter-add.6
  385.9 204.5 %all-gather.14.cloned.1.call-done = f32[512,128,128]{2,1,0:T(8,128)} async-done(((f32[16,128,128]{2,1,0:T(8,128)}), f32[512,128,128]{2,1,0:T(8,128)}) %all-gather.14.cloned.1.call-update) | async-done | bytes 33554448 | tf_op jit(solution)/shard_map/all_gather | solution.py:19
  590.6 46.6 %while.66 = (s32[]{:T(128)}, f32[16,128,128]{2,1,0:T(8,128)S(1)}, s32[]{:T(128)}, f32[32,16]{1,0:T(8,128)S(1)}, f32[32,16,128,128]{3,2,1,0:T(8,128)}, /*index=5*/s32[]{:T(128)}, s32[]{:T(128)}, s32[]{:T(128)}) while((s32[]{:T(128)}, f32[16,128,128]{2,1,0:T(8,128)S(1)}, s32[]{:T(128)}, f32[32,16]{1,0:T(8,128)S(1)}, ...), condition=%wide.region_4.5_spmd, body=%wide.region_3.4_spmd.sunk | while | flops 524293 | bytes 3146047 | solution.py:28
  637.1 3.6 fusion.20
  640.7 4.3 fusion.26
  646.5 4.2 fusion.22
  (232 shorter events, 133.4 us)
Async XLA Ops:
  7.2 59.0 %all-gather.16.cloned.1.call-start = ((), (), s32[]{:S(2)}) async-start(), calls=%async_computation.2 | async-start | bytes 9437184 | tf_op jit(solution)/shard_map/all_gather | solution.py:182
  11.1 2.3 copy-start.11
  13.3 1.0 copy-start.12
  13.3 107.1 %all-gather.12.cloned.1.call-start = ((), (), s32[]{:S(2)}) async-start(), calls=%async_computation | async-start | bytes 9437184 | tf_op jit(solution)/shard_map/all_gather | solution.py:181
  14.6 2.3 copy-start.17
  16.8 341.3 %all-gather.18.cloned.1.call-start = ((), (), s32[]{:S(2)}) async-start(), calls=%async_computation.3 | async-start | bytes 34603008 | tf_op jit(solution)/shard_map/all_gather | solution.py:19
  92.5 498.0 %all-gather.14.cloned.1.call-start = ((), (), s32[]{:S(2)}) async-start(), calls=%async_computation.1 | async-start | bytes 34603008 | tf_op jit(solution)/shard_map/all_gather | solution.py:19
  146.3 8.1 %copy-start.16 = (u32[256]{0:T(256)S(1)}, u32[256]{0:T(256)}, u32[]{:S(2)}) copy-start(u32[256]{0:T(256)} %constant.203) | copy-start | bytes 3076
  148.0 14.6 %collective-permute-start.1 = (bf16[64,16,128]{2,0,1:T(8,128)(2,1)}, bf16[64,16,128]{2,0,1:T(8,128)(2,1)}, u32[]{:S(2)}, u32[]{:S(2)}) collective-permute-start(bf16[64,16,128]{2,0,1:T(8,128)(2,1)} %copy_bitcast_fusion), channel_id=1, source_target_pairs={{0,1},{1,2},{2,3},{3,4},{4,5},{5,6},{6,7},{7,8},{8,9},{9,10},{10,1... | collective-permute-start | bytes 786440 | tf_op jit(solution)/shard_map/ppermute | solution.py:12
  151.2 22.1 %collective-permute-start = (bf16[64,16,128]{2,0,1:T(8,128)(2,1)S(1)}, bf16[64,16,128]{2,0,1:T(8,128)(2,1)}, u32[]{:S(2)}, u32[]{:S(2)}) collective-permute-start(bf16[64,16,128]{2,0,1:T(8,128)(2,1)S(1)} %copy_bitcast_fusion.1), channel_id=1, source_target_pairs={{0,1},{1,2},{2,3},{3,4},{4,5},{5,6},{6,7},{7,8},{8,9},{9,10},{10,1... | collective-permute-start | bytes 786440 | tf_op jit(solution)/shard_map/ppermute | solution.py:12
  154.0 11.2 %copy-start.15 = (bf16[128,16,128]{2,0,1:T(8,128)(2,1)}, bf16[128,16,128]{2,0,1:T(8,128)(2,1)S(1)}, u32[]{:S(2)}) copy-start(bf16[128,16,128]{2,0,1:T(8,128)(2,1)S(1)} %copy.84) | copy-start | bytes 1572868
  154.3 19.0 %copy-start.5 = (bf16[128,16,128]{2,0,1:T(8,128)(2,1)}, bf16[128,16,128]{2,0,1:T(8,128)(2,1)S(1)}, u32[]{:S(2)}) copy-start(bf16[128,16,128]{2,0,1:T(8,128)(2,1)S(1)} %copy.82) | copy-start | bytes 1572868
  156.4 2.1 copy-start.9
  157.0 3.0 copy-start.7
  170.8 191.5 %collective-permute-start.3 = (bf16[64,16,128]{0,2,1:T(8,128)(2,1)}, bf16[64,16,128]{0,2,1:T(8,128)(2,1)}, u32[]{:S(2)}, u32[]{:S(2)}) collective-permute-start(bf16[64,16,128]{0,2,1:T(8,128)(2,1)} %slice.107), channel_id=1, source_target_pairs={{1,0},{2,1},{3,2},{4,3},{5,4},{6,5},{7,6},{8,7},{9,8},{10,9},{11,1... | collective-permute-start | bytes 786440 | tf_op jit(solution)/shard_map/ppermute | solution.py:12
  182.8 195.6 %collective-permute-start.2 = (bf16[64,16,128]{0,2,1:T(8,128)(2,1)}, bf16[64,16,128]{0,2,1:T(8,128)(2,1)}, u32[]{:S(2)}, u32[]{:S(2)}) collective-permute-start(bf16[64,16,128]{0,2,1:T(8,128)(2,1)} %slice.108), channel_id=1, source_target_pairs={{1,0},{2,1},{3,2},{4,3},{5,4},{6,5},{7,6},{8,7},{9,8},{10,9},{11,1... | collective-permute-start | bytes 786440 | tf_op jit(solution)/shard_map/ppermute | solution.py:12
  358.5 3.4 copy-start.10
  358.5 3.4 copy-start.14
  362.3 1.0 copy-start.2
  375.1 2.8 copy-start.8
  375.1 2.8 copy-start.13
  590.6 46.6 %copy-start.4 = (f32[128,16,128]{0,2,1:T(8,128)S(1)}, f32[128,16,128]{0,2,1:T(8,128)}, u32[]{:S(2)}) copy-start(f32[128,16,128]{0,2,1:T(8,128)} %convolution_bitcast_fusion.7) | copy-start | bytes 3145732
  645.0 1.4 copy-start.3
  646.5 4.2 copy-start.6
  (2 other events, 1.9 us)
Sparse Core Ops, SparseCore 0:
  13.5 52.6 all-gather.15
  68.0 52.3 all-gather.11
  123.0 235.1 all-gather.17
  360.6 229.8 all-gather.13
where the time goes:
time: 664 us; the launch traced here: 661 us
  waiting for transfers between devices  368 us (55%)
  other arithmetic  92.1 us (14%)
  blocking collectives  87.6 us (13%)
  matrix products  43.3 us (7%)
  local copies, waits for them, and re-layouts  43.1 us (6%)
  between operations  15.6 us (2%)
  starting transfers between devices  9.56 us (1%)
    all_gather x2, waiting for transfers between devices, carried_in(): gathered = jax.tree.map(lambda a: lax.all_gather(a, axis), part)  305 us
    unnamed x2, blocking collectives  87.6 us
    add x39, other arithmetic, forward_merge(): later_part[0][:, None, None] * earlier_part[1] + later_part[1]  56.4 us
    all_gather x1, waiting for transfers between devices, per_device(): lax.all_gather(grad_local[None], 'inner', axis=0, tiled=True)  32.2 us
    all_gather x1, waiting for transfers between devices, per_device(): lax.all_gather(state_local[None], 'inner', axis=0, tiled=True)  27.8 us
    dot_general x11, matrix products, low_product(): return jnp.einsum(form, left, right, preferred_element_type=jnp.float32)  22.3 us
    dot_general x6, matrix products, high_product(): return jnp.einsum(form, left, right, precision=lax.Precision.HIGHEST)  18.3 us
    dynamic_update_slice x16, other arithmetic, per_device(): lax.scan(run_forward, identity_pair, (group_decay, group_state))  17.3 us
  transfers between devices with their start and end apart: 8, of which 5 were waited for; matrix products, arithmetic and copies ran while one was open for 16% of the time, Pallas kernels for 0%

commit v1 on v0

v1 whole, which is shorter than its diff:
```python
import jax
import jax.numpy as jnp
from jax import lax
from jax.experimental import pallas as pl
from jax.experimental.pallas import tpu as pltpu
from jax.sharding import Mesh
from jax.sharding import PartitionSpec as P

AXES = ("z", "x", "y", "c")
GRID = (8, 4, 4, 2)
PLANE = 16
W = 64
DH = 128
HALF = 8
COLS = HALF * DH
MSG = 144
F32 = jnp.float32
BF16 = jnp.bfloat16


def dot(a, b, ca, cb):
    return lax.dot_general(a, b, (((ca,), (cb,)), ((), ())), preferred_element_type=F32)


def cumulative(gates):
    n = gates.shape[1]
    i = lax.broadcasted_iota(jnp.int32, (n, n), 0)
    j = lax.broadcasted_iota(jnp.int32, (n, n), 1)
    upper = (i <= j).astype(F32)
    rows = lax.dot_general(gates, upper, (((1,), (0,)), ((), ())), precision=lax.Precision.HIGHEST, preferred_element_type=F32)
    return rows, rows.T


def decay_tile(d):
    d = jnp.broadcast_to(d, (16, DH))
    hi = d.astype(BF16).astype(F32)
    mid = (d - hi).astype(BF16).astype(F32)
    low = d - hi - mid
    row = lax.broadcasted_iota(jnp.int32, (16, DH), 0)
    zero = jnp.zeros_like(d)
    return jnp.where(row == 0, hi, jnp.where(row == 1, mid, jnp.where(row == 2, low, zero))).astype(BF16)


def decay_of(tile):
    return jnp.sum(tile.astype(F32), axis=0, keepdims=True)


def states_kernel(sel_ref, q_ref, k_ref, v_ref, g_ref, gate_ref, msg_ref):
    rows, cols = cumulative(gate_ref[...])
    for j in range(HALF):
        at = slice(j * DH, (j + 1) * DH)
        last = rows[j : j + 1, DH - 1 : DH]
        head = jnp.exp(cols[:, j : j + 1])
        tail = jnp.exp(last - cols[:, j : j + 1])
        kt = (k_ref[:, at].astype(F32) * tail).astype(BF16)
        qh = (q_ref[:, at].astype(F32) * head).astype(BF16)
        s = dot(kt, v_ref[:, at], 0, 0).astype(BF16)
        g = dot(qh, g_ref[:, at], 0, 0).astype(BF16)
        d = decay_tile(jnp.exp(last))
        for r in range(2):
            part = slice(r * 64, (r + 1) * 64)
            msg_ref[2 * j + r, 0:64, :] = s[part]
            msg_ref[2 * j + r, 64:128, :] = g[part]
            msg_ref[2 * j + r, 128:144, :] = d


def combine_kernel(c_ref, own_ref, other_ref, out_ref):
    first = c_ref[0] == 0

    def body(a_ref, b_ref):
        for p in range(PLANE):
            da = decay_of(a_ref[p, 128:144, :])
            db = decay_of(b_ref[p, 128:144, :])
            out_ref[p, 0:64, :] = (db * a_ref[p, 0:64, :].astype(F32) + b_ref[p, 0:64, :].astype(F32)).astype(BF16)
            out_ref[p, 64:128, :] = (a_ref[p, 64:128, :].astype(F32) + da * b_ref[p, 64:128, :].astype(F32)).astype(BF16)
            out_ref[p, 128:144, :] = decay_tile(da * db)

    @pl.when(first)
    def _():
        body(own_ref, other_ref)

    @pl.when(jnp.logical_not(first))
    def _():
        body(other_ref, own_ref)


def plane_kernel(msg_ref, out_ref):
    fwd = jnp.zeros((64, DH), F32)
    bwd = jnp.zeros((64, DH), F32)
    d = jnp.ones((1, DH), F32)
    for p in range(PLANE):
        b = PLANE - 1 - p
        dp = decay_of(msg_ref[p, 128:144, :])
        fwd = dp * fwd + msg_ref[p, 0:64, :].astype(F32)
        bwd = decay_of(msg_ref[b, 128:144, :]) * bwd + msg_ref[b, 64:128, :].astype(F32)
        d = d * dp
    tile = decay_tile(d)
    for z in range(GRID[0]):
        out_ref[z, 0:64, :] = fwd.astype(BF16)
        out_ref[z, 64:128, :] = bwd.astype(BF16)
        out_ref[z, 128:144, :] = tile


def incoming_kernel(z_ref, msg_ref, planes_ref, out_ref):
    z = z_ref[0]
    n = GRID[0]
    fwd = jnp.zeros((64, DH), F32)
    bwd = jnp.zeros((64, DH), F32)
    for i in range(n):
        b = n - 1 - i
        new_f = decay_of(planes_ref[i, 128:144, :]) * fwd + planes_ref[i, 0:64, :].astype(F32)
        fwd = jnp.where(i < z, new_f, fwd)
        new_b = decay_of(planes_ref[b, 128:144, :]) * bwd + planes_ref[b, 64:128, :].astype(F32)
        bwd = jnp.where(b > z, new_b, bwd)
    for p in range(PLANE):
        b = PLANE - 1 - p
        out_ref[p, 0:64, :] = fwd.astype(BF16)
        out_ref[b, 64:128, :] = bwd.astype(BF16)
        fwd = decay_of(msg_ref[p, 128:144, :]) * fwd + msg_ref[p, 0:64, :].astype(F32)
        bwd = decay_of(msg_ref[b, 128:144, :]) * bwd + msg_ref[b, 64:128, :].astype(F32)


def hand_kernel(c_ref, chip_ref, own_ref, other_ref, mine_ref, theirs_ref):
    first = c_ref[0] == 0

    def body(is_first):
        for p in range(PLANE):
            fwd = chip_ref[p, 0:64, :]
            bwd = chip_ref[p, 64:128, :]
            inner = own_ref if is_first else other_ref
            outer = other_ref if is_first else own_ref
            late_f = (decay_of(inner[p, 128:144, :]) * fwd.astype(F32) + inner[p, 0:64, :].astype(F32)).astype(BF16)
            early_b = (decay_of(outer[p, 128:144, :]) * bwd.astype(F32) + outer[p, 64:128, :].astype(F32)).astype(BF16)
            early_ref = mine_ref if is_first else theirs_ref
            late_ref = theirs_ref if is_first else mine_ref
            early_ref[p, 0:64, :] = fwd
            early_ref[p, 64:128, :] = early_b
            late_ref[p, 0:64, :] = late_f
            late_ref[p, 64:128, :] = bwd

    @pl.when(first)
    def _():
        body(True)

    @pl.when(jnp.logical_not(first))
    def _():
        body(False)


def window_kernel(lin_scale, live_ref, q_ref, k_ref, v_ref, g_ref, halo_ref, gate_ref, o_ref, qg_ref, kg_ref, vg_ref, back_ref):
    live = live_ref[0] > 0
    rows, cols = cumulative(gate_ref[...])
    t = lax.broadcasted_iota(jnp.int32, (DH, DH), 0)
    lane = lax.broadcasted_iota(jnp.int32, (DH, DH), 1)
    key = jnp.where(t < W, lane - W, lane)
    causal = (key >= 0) & (key <= t)
    banded = (key > t - W) & (key <= t) & ((key >= 0) | live)
    scale = DH**-0.5
    for j in range(HALF):
        at = slice(j * DH, (j + 1) * DH)
        q, k, v, g = q_ref[:, at], k_ref[:, at], v_ref[:, at], g_ref[:, at]
        kx = jnp.concatenate([halo_ref[0:W, at], k[0:W]], axis=0)
        vx = jnp.concatenate([halo_ref[W : 2 * W, at], v[0:W]], axis=0)
        a = jnp.concatenate([dot(q[0:W], kx, 1, 1), dot(q[W:], k, 1, 1)], axis=0)
        b = jnp.concatenate([dot(g[0:W], vx, 1, 1), dot(g[W:], v, 1, 1)], axis=0)
        row = rows[j : j + 1, :]
        shifted = jnp.concatenate([row[:, W:], row[:, :W]], axis=1)
        gap = cols[:, j : j + 1] - jnp.where(t < W, shifted, row)
        decay = jnp.where(causal, jnp.exp(jnp.minimum(gap, 0.0)), 0.0) * lin_scale
        logits = jnp.where(banded, a * scale, -jnp.inf)
        e = jnp.exp(logits - jnp.max(logits, axis=1, keepdims=True))
        prob = e / jnp.sum(e, axis=1, keepdims=True)
        delta = jnp.sum(prob * b, axis=1, keepdims=True)
        w1 = (prob + decay * a).astype(BF16)
        w2 = (prob * (b - delta) * scale + decay * b).astype(BF16)
        o_ref[0:W, at] = dot(w1[0:W], vx, 1, 0)
        o_ref[W:, at] = dot(w1[W:], v, 1, 0)
        qg_ref[0:W, at] = dot(w2[0:W], kx, 1, 0)
        qg_ref[W:, at] = dot(w2[W:], k, 1, 0)
        k_top = dot(w2[0:W], q[0:W], 0, 0)
        k_low = dot(w2[W:], q[W:], 0, 0)
        v_top = dot(w1[0:W], g[0:W], 0, 0)
        v_low = dot(w1[W:], g[W:], 0, 0)
        kg_ref[0:W, at] = k_low[0:W] + k_top[W:]
        kg_ref[W:, at] = k_low[W:]
        vg_ref[0:W, at] = v_low[0:W] + v_top[W:]
        vg_ref[W:, at] = v_low[W:]
        back_ref[0:W, at] = k_top[0:W].astype(BF16)
        back_ref[W : 2 * W, at] = v_top[0:W].astype(BF16)


def final_kernel(lin_scale, n_alias, sel_ref, q_ref, k_ref, v_ref, g_ref, ret_ref, gate_ref, st_ref, po_ref, pq_ref, pk_ref, pv_ref, *rest):
    o_ref, qg_ref, kg_ref, vg_ref = rest[n_alias:]
    rows, cols = cumulative(gate_ref[...])
    for j in range(HALF):
        at = slice(j * DH, (j + 1) * DH)
        last = rows[j : j + 1, DH - 1 : DH]
        head = jnp.exp(cols[:, j : j + 1]) * lin_scale
        tail = jnp.exp(last - cols[:, j : j + 1]) * lin_scale
        s = jnp.concatenate([st_ref[2 * j, 0:64, :], st_ref[2 * j + 1, 0:64, :]], axis=0)
        m = jnp.concatenate([st_ref[2 * j, 64:128, :], st_ref[2 * j + 1, 64:128, :]], axis=0)
        o_ref[:, at] = (po_ref[:, at] + head * dot(q_ref[:, at], s, 1, 0)).astype(BF16)
        qg_ref[:, at] = (pq_ref[:, at] + head * dot(g_ref[:, at], s, 1, 1)).astype(BF16)
        kg = pk_ref[:, at] + tail * dot(v_ref[:, at], m, 1, 1)
        vg = pv_ref[:, at] + tail * dot(k_ref[:, at], m, 1, 0)
        kg_ref[0:W, at] = kg[0:W].astype(BF16)
        kg_ref[W:, at] = (kg[W:] + ret_ref[0:W, at].astype(F32)).astype(BF16)
        vg_ref[0:W, at] = vg[0:W].astype(BF16)
        vg_ref[W:, at] = (vg[W:] + ret_ref[W : 2 * W, at].astype(F32)).astype(BF16)


def cost(flops, nbytes):
    return pl.CostEstimate(flops=int(flops), bytes_accessed=int(nbytes), transcendentals=0)


def half_specs(n):
    return [pl.BlockSpec((128, COLS), lambda i, sel: (0, sel[0])) for _ in range(n)]


GATE = pl.BlockSpec((HALF, DH), lambda i, sel: (sel[0], 0))


def whole(shape):
    return pl.BlockSpec(shape, lambda *_: (0,) * len(shape))


def local_states(sel, q, k, v, g, gates):
    return pl.pallas_call(
        states_kernel,
        out_shape=jax.ShapeDtypeStruct((PLANE, MSG, DH), BF16),
        grid_spec=pltpu.PrefetchScalarGridSpec(
            num_scalar_prefetch=1, grid=(1,), in_specs=half_specs(4) + [GATE], out_specs=whole((PLANE, MSG, DH))
        ),
        cost_estimate=cost(7e7, 1.6e6),
        name="local_states",
    )(sel, q, k, v, g, gates)


def small_call(body, name, scalar, arrays, outs):
    return pl.pallas_call(
        body,
        out_shape=tuple(jax.ShapeDtypeStruct(s, BF16) for s in outs),
        grid_spec=pltpu.PrefetchScalarGridSpec(
            num_scalar_prefetch=1,
            grid=(1,),
            in_specs=[whole(a.shape) for a in arrays],
            out_specs=tuple(whole(s) for s in outs),
        ),
        cost_estimate=cost(1e6, 2e6),
        name=name,
    )(scalar, *arrays)


def window(lin_scale, live, q, k, v, g, halo, gates):
    col = pl.BlockSpec((128, COLS), lambda i, s: (0, i))
    return pl.pallas_call(
        lambda *refs: window_kernel(lin_scale, *refs),
        out_shape=tuple(jax.ShapeDtypeStruct((128, 2048), F32) for _ in range(4)) + (jax.ShapeDtypeStruct((128, 2048), BF16),),
        grid_spec=pltpu.PrefetchScalarGridSpec(
            num_scalar_prefetch=1,
            grid=(2,),
            in_specs=[col] * 5 + [pl.BlockSpec((HALF, DH), lambda i, s: (i, 0))],
            out_specs=(col,) * 5,
        ),
        cost_estimate=cost(6e8, 8e6),
        name="window",
    )(live, q, k, v, g, halo, gates)


def finish(lin_scale, sel, q, k, v, g, ret, gates, states, parts, previous):
    n = len(previous)
    return pl.pallas_call(
        lambda *refs: final_kernel(lin_scale, n, *refs),
        out_shape=tuple(jax.ShapeDtypeStruct((128, 2048), BF16) for _ in range(4)),
        grid_spec=pltpu.PrefetchScalarGridSpec(
            num_scalar_prefetch=1,
            grid=(1,),
            in_specs=half_specs(5)
            + [GATE, whole(states.shape)]
            + half_specs(4)
            + [pl.BlockSpec(memory_space=pl.ANY)] * n,
            out_specs=tuple(half_specs(4)),
        ),
        input_output_aliases={12 + i: i for i in range(n)},
        cost_estimate=cost(3e8, 5e6),
        name="finish",
    )(sel, q, k, v, g, ret, gates, states, *parts, *previous)


def per_device(q, k, v, g, gates):
    lin_scale = (DH * q.shape[0] * 256) ** (-0.5)
    core = lax.axis_index("c")
    mine = core[None].astype(jnp.int32)
    theirs = 1 - mine
    z = lax.axis_index("z")[None].astype(jnp.int32)
    live = (lax.axis_index(AXES) > 0)[None].astype(jnp.int32)
    swap = [(0, 1), (1, 0)]

    sent = local_states(theirs, q, k, v, g, gates)
    other = lax.ppermute(sent, "c", swap)
    own = local_states(mine, q, k, v, g, gates)
    (chip,) = small_call(combine_kernel, "combine", mine, (own, other), [(PLANE, MSG, DH)])
    plane = lax.all_to_all(chip, ("x", "y"), 0, 0, tiled=True)

    halo = lax.ppermute(jnp.concatenate([k[-W:], v[-W:]], axis=0), AXES, [(i, i + 1) for i in range(255)])
    *parts, back = window(lin_scale, live, q, k, v, g, halo, gates)
    ret = lax.ppermute(back, AXES, [(i + 1, i) for i in range(255)])

    (total,) = small_call(lambda s, m, o: plane_kernel(m, o), "plane", z, (plane,), [(GRID[0], MSG, DH)])
    planes = lax.all_to_all(total, "z", 0, 0, tiled=True)
    (incoming,) = small_call(incoming_kernel, "incoming", z, (plane, planes), [(PLANE, DH, DH)])
    chip_in = lax.all_to_all(incoming, ("x", "y"), 0, 0, tiled=True)
    st_mine, st_theirs = small_call(hand_kernel, "hand", mine, (chip_in, own, other), [(PLANE, DH, DH)] * 2)
    st_other = lax.ppermute(st_theirs, "c", swap)
    outs = finish(lin_scale, mine, q, k, v, g, ret, gates, st_mine, parts, ())
    outs = finish(lin_scale, theirs, q, k, v, g, ret, gates, st_other, parts, outs)
    return outs


def solution(mesh):
    fine = Mesh(mesh.devices.reshape(GRID), AXES)
    rows = P(AXES, None)
    return jax.shard_map(
        per_device,
        mesh=fine,
        in_specs=(rows,) * 4 + (P(None, AXES),),
        out_specs=(rows,) * 4,
        check_vma=False,
    )
```

time: 664 us -> 95.8 us (0.14)
  the two profiles are of different devices: /device:TPU:230 before, /device:TPU:31 now
where the time goes in v1:
time: 95.8 us; the launch traced here: 95.1 us
  Pallas kernels  36.1 us (38%)
  starting transfers between devices  35.9 us (37%)
  waiting for transfers between devices  15.9 us (17%)
  local copies, waits for them, and re-layouts  6.56 us (7%)
    pallas_call x1, Pallas kernels, window(): pl.pallas_call(lambda *refs: window_kernel(lin_scale, *refs), out_shape=t...  12.3 us
    pallas_call x4, Pallas kernels, small_call(): pl.pallas_call(body, out_shape=tuple((jax.ShapeDtypeStruct(s, BF16) for s...  9 us
    ppermute x1, starting transfers between devices, per_device(): lax.ppermute(jnp.concatenate([k[-W:], v[-W:]], axis=0), AXES, [(i, i + 1)...  8.41 us
    all_to_all x1, waiting for transfers between devices, per_device(): plane = lax.all_to_all(chip, ('x', 'y'), 0, 0, tiled=True)  8.4 us
    all_to_all x1, starting transfers between devices, per_device(): planes = lax.all_to_all(total, 'z', 0, 0, tiled=True)  8.19 us
    pallas_call x2, Pallas kernels, finish(): pl.pallas_call(lambda *refs: final_kernel(lin_scale, n, *refs), out_shape...  8.06 us
    all_to_all x1, starting transfers between devices, per_device(): chip_in = lax.all_to_all(incoming, ('x', 'y'), 0, 0, tiled=True)  6.76 us
    pallas_call x2, Pallas kernels, local_states(): pl.pallas_call(states_kernel, out_shape=jax.ShapeDtypeStruct((PLANE, MSG,...  6.71 us
  transfers between devices with their start and end apart: 7, of which 3 were waited for; matrix products, arithmetic and copies ran while one was open for 0% of the time, Pallas kernels for 26%

profile of v1, /device:TPU:31, one launch (start us, length us, event | category | flops | bytes accessed | tf_op | source)
XLA Modules:
  0.0 95.1 jit_solution(14643740227646357663)
XLA Ops:
  0.6 3.4 %local_states.3 = bf16[16,144,128]{2,1,0:T(8,128)(2,1)} custom-call(s32[1]{0:T(128)S(6)} %sub.3.sel_ref.refs_0_, bf16[128,2048]{1,0:T(8,128)(2,1)} %refs_1_.5, bf16[128,2048]{1,0:T(8,128)(2,1)} %refs_2_.5, bf16[128,2048]{1,0:T(8,128)(2,1)} %refs_3_.5, bf16[128,2048]{1,0:T(8,128)(2,1)} %refs_4_.5, f32[16,128]{1,0:T(8,128)} %refs_6_.5), custom_call_target="tpu_custom_call" | custom-call | flops 70000000 | bytes 1600000 | tf_op jit(solution)/shard_map/local_states/pallas_call | solution.py:228
  4.7 3.3 %local_states.2.own_ref = bf16[16,144,128]{2,1,0:T(8,128)(2,1)} custom-call(s32[1]{0:T(128)} %bitcast.sel_ref.c_ref.refs_0_, bf16[128,2048]{1,0:T(8,128)(2,1)} %refs_1_.5, bf16[128,2048]{1,0:T(8,128)(2,1)} %refs_2_.5, bf16[128,2048]{1,0:T(8,128)(2,1)} %refs_3_.5, bf16[128,2048]{1,0:T(8,128)(2,1)} %refs_4_.5, f32[16,128]{1,0:T(8,128)} %refs_6_.5), custom_call_target="tpu_custom_call" | custom-call | flops 70000000 | bytes 1600000 | tf_op jit(solution)/shard_map/local_states/pallas_call | solution.py:228
  8.0 0.8 copy-done.1
  8.9 2.3 %combine.1 = bf16[16,144,128]{2,1,0:T(8,128)(2,1)} custom-call(s32[1]{0:T(128)} %bitcast.sel_ref.c_ref.refs_0_, bf16[16,144,128]{2,1,0:T(8,128)(2,1)} %local_states.2.own_ref, bf16[16,144,128]{2,1,0:T(8,128)(2,1)} %copy-done.1), custom_call_target="tpu_custom_call" | custom-call | flops 1000000 | bytes 2000000 | tf_op jit(solution)/shard_map/combine/pallas_call | solution.py:240
  11.2 6.5 %all-to-all-start = ((bf16[16,144,128]{2,1,0:T(8,128)(2,1)}), bf16[16,144,128]{2,1,0:T(8,128)(2,1)S(1)}, u32[]{:S(2)}, u32[]{:S(2)}) async-start(bf16[16,144,128]{2,1,0:T(8,128)(2,1)} %combine.1), calls=%async_computation | async-start | bytes 1179648 | tf_op jit(solution)/shard_map/all_to_all | solution.py:303
  17.7 8.4 %all-to-all-done.m.msg_ref = bf16[16,144,128]{2,1,0:T(8,128)(2,1)S(1)} async-done(((bf16[16,144,128]{2,1,0:T(8,128)(2,1)}), bf16[16,144,128]{2,1,0:T(8,128)(2,1)S(1)}, u32[]{:S(2)}, u32[]{:S(2)}) %all-to-all-start) | async-done | bytes 589856 | tf_op jit(solution)/shard_map/all_to_all | solution.py:303
  26.1 0.8 copy-done
  26.9 1.9 %plane.1 = bf16[8,144,128]{2,1,0:T(8,128)(2,1)} custom-call(s32[1]{0:T(128)} %bitcast.2.s.z_ref, bf16[16,144,128]{2,1,0:T(8,128)(2,1)} %copy-done), custom_call_target="tpu_custom_call" | custom-call | flops 1000000 | bytes 2000000 | tf_op jit(solution)/shard_map/plane/pallas_call | solution.py:240
  28.8 8.2 %all-to-all-start.1 = ((bf16[8,144,128]{2,1,0:T(8,128)(2,1)}), bf16[8,144,128]{2,1,0:T(8,128)(2,1)S(1)}, u32[]{:S(2)}, u32[]{:S(2)}) async-start(bf16[8,144,128]{2,1,0:T(8,128)(2,1)} %plane.1), calls=%async_computation.1 | async-start | bytes 589824 | tf_op jit(solution)/shard_map/all_to_all | solution.py:310
  37.0 0.9 slice-done
  38.1 8.4 %collective-permute-start = (bf16[128,2048]{1,0:T(8,128)(2,1)S(1)}, bf16[128,2048]{1,0:T(8,128)(2,1)S(1)}, u32[]{:S(2)}, u32[]{:S(2)}) collective-permute-start(bf16[128,2048]{1,0:T(8,128)(2,1)S(1)} %pad_maximum_fusion), channel_id=1, source_target_pairs={{0,1},{1,2},{2,3},{3,4},{4,5},{5,6},{6,7},{7,8},{8,9},{9,10},{10,1... | collective-permute-start | bytes 1572872 | tf_op jit(solution)/shard_map/ppermute | solution.py:305
  46.5 1.3 %all-to-all-done.1.planes_ref = bf16[8,144,128]{2,1,0:T(8,128)(2,1)S(1)} async-done(((bf16[8,144,128]{2,1,0:T(8,128)(2,1)}), bf16[8,144,128]{2,1,0:T(8,128)(2,1)S(1)}, u32[]{:S(2)}, u32[]{:S(2)}) %all-to-all-start.1) | async-done | bytes 294944 | tf_op jit(solution)/shard_map/all_to_all | solution.py:310
  48.5 2.2 %incoming.1 = bf16[16,128,128]{2,1,0:T(8,128)(2,1)} custom-call(s32[1]{0:T(128)} %bitcast.2.s.z_ref, bf16[16,144,128]{2,1,0:T(8,128)(2,1)} %copy-done, bf16[8,144,128]{2,1,0:T(8,128)(2,1)} %copy-done.4), custom_call_target="tpu_custom_call" | custom-call | flops 1000000 | bytes 2000000 | tf_op jit(solution)/shard_map/incoming/pallas_call | solution.py:240
  50.7 6.8 %all-to-all-start.2 = ((bf16[16,128,128]{2,1,0:T(8,128)(2,1)}), bf16[16,128,128]{2,1,0:T(8,128)(2,1)S(1)}, u32[]{:S(2)}, u32[]{:S(2)}) async-start(bf16[16,128,128]{2,1,0:T(8,128)(2,1)} %incoming.1), calls=%async_computation.2 | async-start | bytes 1048576 | tf_op jit(solution)/shard_map/all_to_all | solution.py:312
  57.5 0.8 copy-done.6
  58.3 12.3 %window.1 = (f32[128,2048]{1,0:T(8,128)}, f32[128,2048]{1,0:T(8,128)}, f32[128,2048]{1,0:T(8,128)}, f32[128,2048]{1,0:T(8,128)}, bf16[128,2048]{1,0:T(8,128)(2,1)}) custom-call(s32[1]{0:T(128)} %bitcast.1.refs_0_, bf16[128,2048]{1,0:T(8,128)(2,1)} %refs_1_.5, bf16[128,2048]{1,0:T(8,128)(2,1)} %refs_2_.5, bf16[128,2048]{1,0:T(8,128)(2,1)} %refs_3_.5, ...), custom_call_target="tpu_custom_call" | custom-call | flops 600000000 | bytes 8000000 | tf_op jit(solution)/shard_map/window/pallas_call | solution.py:256
  70.6 5.3 %collective-permute-start.1 = (bf16[128,2048]{1,0:T(8,128)(2,1)}, bf16[128,2048]{1,0:T(8,128)(2,1)S(1)}, u32[]{:S(2)}, u32[]{:S(2)}) collective-permute-start(bf16[128,2048]{1,0:T(8,128)(2,1)} %get-tuple-element.15), channel_id=1, source_target_pairs={{1,0},{2,1},{3,2},{4,3},{5,4},{6,5},{7,6},{8,7},{9,8},{10,9},{11,1... | collective-permute-start | bytes 1572872 | tf_op jit(solution)/shard_map/ppermute | solution.py:307
  75.9 0.8 copy-done.3
  76.7 2.6 %hand.1 = (bf16[16,128,128]{2,1,0:T(8,128)(2,1)}, bf16[16,128,128]{2,1,0:T(8,128)(2,1)}) custom-call(s32[1]{0:T(128)} %bitcast.sel_ref.c_ref.refs_0_, bf16[16,128,128]{2,1,0:T(8,128)(2,1)} %copy-done.3, bf16[16,144,128]{2,1,0:T(8,128)(2,1)} %local_states.2.own_ref, bf16[16,144,128]{2,1,0:T(8,128)(2,1)} %copy-done.1), custom_call_target="tpu_custom_call" | custom-call | flops 1000000 | bytes 2000000 | tf_op jit(solution)/shard_map/hand/pallas_call | solution.py:240
  79.3 6.2 %collective-permute-done.1.refs_5_ = bf16[128,2048]{1,0:T(8,128)(2,1)S(1)} collective-permute-done((bf16[128,2048]{1,0:T(8,128)(2,1)}, bf16[128,2048]{1,0:T(8,128)(2,1)S(1)}, u32[]{:S(2)}, u32[]{:S(2)}) %collective-permute-start.1) | collective-permute-done | bytes 524320 | tf_op jit(solution)/shard_map/ppermute | solution.py:307
  85.5 0.8 copy-done.2
  86.3 4.0 %finish.2 = (bf16[128,2048]{1,0:T(8,128)(2,1)}, bf16[128,2048]{1,0:T(8,128)(2,1)}, bf16[128,2048]{1,0:T(8,128)(2,1)}, bf16[128,2048]{1,0:T(8,128)(2,1)}) custom-call(s32[1]{0:T(128)} %bitcast.sel_ref.c_ref.refs_0_, bf16[128,2048]{1,0:T(8,128)(2,1)} %refs_1_.5, bf16[128,2048]{1,0:T(8,128)(2,1)} %refs_2_.5, bf16[128,2048]{1,0:T(8,128)(2,1)} %refs_3_.5, ...), custom_call_target="tpu_custom_call" | custom-call | flops 300000000 | bytes 5000000 | tf_op jit(solution)/shard_map/finish/pallas_call | solution.py:272
  90.3 0.8 copy-done.5
  91.1 4.0 %finish.3 = (bf16[128,2048]{1,0:T(8,128)(2,1)}, bf16[128,2048]{1,0:T(8,128)(2,1)}, bf16[128,2048]{1,0:T(8,128)(2,1)}, bf16[128,2048]{1,0:T(8,128)(2,1)}) custom-call(s32[1]{0:T(128)S(6)} %sub.3.sel_ref.refs_0_, bf16[128,2048]{1,0:T(8,128)(2,1)} %refs_1_.5, ...), custom_call_target="tpu_custom_call", output_to_operand_aliasing={{0}: (12, {}), {1}: (13, {}), {2}: (14, {}), {3}: (15, {})} | custom-call | flops 300000000 | bytes 5000000 | tf_op jit(solution)/shard_map/finish/pallas_call | solution.py:272
  (18 shorter events, 1.6 us)
Async XLA Ops:
  4.0 4.0 %collective-permute-start.2 = (bf16[16,144,128]{2,1,0:T(8,128)(2,1)}, bf16[16,144,128]{2,1,0:T(8,128)(2,1)S(1)}, u32[]{:S(2)}, u32[]{:S(2)}) collective-permute-start(bf16[16,144,128]{2,1,0:T(8,128)(2,1)} %local_states.3), channel_id=1, source_target_pairs={{0,1},{1,0},{2,3},{3,2},{4,5},{5,4},{6,7},{7,6},{8,9},{9,8},{10,11... | collective-permute-start | bytes 1769480 | tf_op jit(solution)/shard_map/ppermute | solution.py:300
  8.0 0.8 copy-start.1
  11.2 14.9 %all-to-all-start = ((bf16[16,144,128]{2,1,0:T(8,128)(2,1)}), bf16[16,144,128]{2,1,0:T(8,128)(2,1)S(1)}, u32[]{:S(2)}, u32[]{:S(2)}) async-start(bf16[16,144,128]{2,1,0:T(8,128)(2,1)} %combine.1), calls=%async_computation | async-start | bytes 1179648 | tf_op jit(solution)/shard_map/all_to_all | solution.py:303
  26.1 0.8 copy-start
  28.8 19.0 %all-to-all-start.1 = ((bf16[8,144,128]{2,1,0:T(8,128)(2,1)}), bf16[8,144,128]{2,1,0:T(8,128)(2,1)S(1)}, u32[]{:S(2)}, u32[]{:S(2)}) async-start(bf16[8,144,128]{2,1,0:T(8,128)(2,1)} %plane.1), calls=%async_computation.1 | async-start | bytes 589824 | tf_op jit(solution)/shard_map/all_to_all | solution.py:310
  37.0 0.9 slice-start
  37.0 1.0 %slice-start.1 = ((bf16[128,2048]{1,0:T(8,128)(2,1)}), bf16[64,2048]{1,0:T(8,128)(2,1)S(1)}, s32[]{:S(2)}) async-start(bf16[128,2048]{1,0:T(8,128)(2,1)} %refs_3_.5), calls=%async_computation.4 | async-start | bytes 524288 | tf_op jit(solution)/shard_map/slice | solution.py:305
  38.1 19.4 %collective-permute-start = (bf16[128,2048]{1,0:T(8,128)(2,1)S(1)}, bf16[128,2048]{1,0:T(8,128)(2,1)S(1)}, u32[]{:S(2)}, u32[]{:S(2)}) collective-permute-start(bf16[128,2048]{1,0:T(8,128)(2,1)S(1)} %pad_maximum_fusion), channel_id=1, source_target_pairs={{0,1},{1,2},{2,3},{3,4},{4,5},{5,6},{6,7},{7,8},{8,9},{9,10},{10,1... | collective-permute-start | bytes 1572872 | tf_op jit(solution)/shard_map/ppermute | solution.py:305
  47.8 0.7 copy-start.4
  50.7 25.2 %all-to-all-start.2 = ((bf16[16,128,128]{2,1,0:T(8,128)(2,1)}), bf16[16,128,128]{2,1,0:T(8,128)(2,1)S(1)}, u32[]{:S(2)}, u32[]{:S(2)}) async-start(bf16[16,128,128]{2,1,0:T(8,128)(2,1)} %incoming.1), calls=%async_computation.2 | async-start | bytes 1048576 | tf_op jit(solution)/shard_map/all_to_all | solution.py:312
  57.5 0.8 copy-start.6
  70.6 14.9 %collective-permute-start.1 = (bf16[128,2048]{1,0:T(8,128)(2,1)}, bf16[128,2048]{1,0:T(8,128)(2,1)S(1)}, u32[]{:S(2)}, u32[]{:S(2)}) collective-permute-start(bf16[128,2048]{1,0:T(8,128)(2,1)} %get-tuple-element.15), channel_id=1, source_target_pairs={{1,0},{2,1},{3,2},{4,3},{5,4},{6,5},{7,6},{8,7},{9,8},{10,9},{11,1... | collective-permute-start | bytes 1572872 | tf_op jit(solution)/shard_map/ppermute | solution.py:307
  75.9 0.8 copy-start.3
  79.3 11.0 %collective-permute-start.3 = (bf16[16,128,128]{2,1,0:T(8,128)(2,1)}, bf16[16,128,128]{2,1,0:T(8,128)(2,1)S(1)}, u32[]{:S(2)}, u32[]{:S(2)}) collective-permute-start(bf16[16,128,128]{2,1,0:T(8,128)(2,1)} %get-tuple-element.16), channel_id=1, source_target_pairs={{0,1},{1,0},{2,3},{3,2},{4,5},{5,4},{6,7},{7,6},{8,9},{9,8},{10,11... | collective-permute-start | bytes 1572872 | tf_op jit(solution)/shard_map/ppermute | solution.py:314
  85.5 0.8 copy-start.2
  90.3 0.8 copy-start.5

commit v2 on v1

v2 whole, which is shorter than its diff:
```python
import math

import jax
import jax.numpy as jnp
from jax import lax
from jax.experimental import pallas as pl
from jax.experimental.pallas import tpu as pltpu
from jax.sharding import Mesh
from jax.sharding import PartitionSpec as P


AXES = ("z", "x", "y", "c")
GRID = (8, 4, 4, 2)
PLANE = 16
W = 64
DH = 128
HALF = 8
COLS = HALF * DH
STEP = 2
WSTEP = 4
MSG = 144
F32 = jnp.float32
BF16 = jnp.bfloat16


def dot(a, b, ca, cb):
    return lax.dot_general(a, b, (((ca,), (cb,)), ((), ())), preferred_element_type=F32)


def cumulative(gates):
    n = gates.shape[1]
    i = lax.broadcasted_iota(jnp.int32, (n, n), 0)
    j = lax.broadcasted_iota(jnp.int32, (n, n), 1)
    upper = (i <= j).astype(F32)
    rows = lax.dot_general(gates, upper, (((1,), (0,)), ((), ())), precision=lax.Precision.HIGHEST, preferred_element_type=F32)
    return rows, rows.T


def decay_tile(d):
    d = jnp.broadcast_to(d, (16, DH))
    hi = d.astype(BF16).astype(F32)
    mid = (d - hi).astype(BF16).astype(F32)
    low = d - hi - mid
    row = lax.broadcasted_iota(jnp.int32, (16, DH), 0)
    zero = jnp.zeros_like(d)
    return jnp.where(row == 0, hi, jnp.where(row == 1, mid, jnp.where(row == 2, low, zero))).astype(BF16)


def decay_of(tile):
    return jnp.sum(tile.astype(F32), axis=0, keepdims=True)


def states_kernel(with_halo, sel_ref, q_hbm, k_hbm, v_hbm, g_hbm, gate_hbm, *rest):
    if with_halo:
        msg_ref, halo_ref, q_ref, k_ref, v_ref, g_ref, gate_ref, sems, gate_sem, halo_sem = rest
    else:
        msg_ref, q_ref, k_ref, v_ref, g_ref, gate_ref, sems, gate_sem = rest
    sel = sel_ref[0]
    gate_copy = pltpu.make_async_copy(gate_hbm.at[pl.ds(pl.multiple_of(sel * HALF, HALF), HALF)], gate_ref, gate_sem)
    gate_copy.start()
    copies = []
    for i in range(HALF // STEP):
        source = pl.ds(pl.multiple_of(sel * COLS + i * STEP * DH, STEP * DH), STEP * DH)
        target = slice(i * STEP * DH, (i + 1) * STEP * DH)
        copies.append([
            pltpu.make_async_copy(big.at[:, source], small.at[:, target], sems.at[i, n])
            for n, (big, small) in enumerate(((k_hbm, k_ref), (v_hbm, v_ref), (q_hbm, q_ref), (g_hbm, g_ref)))
        ])
    for step in copies:
        for copy in step:
            copy.start()
    if with_halo:
        halo_copies = [
            pltpu.make_async_copy(big.at[W : 2 * W], halo_ref.at[n * W : (n + 1) * W], halo_sem.at[n])
            for n, big in enumerate((k_hbm, v_hbm))
        ]
        for copy in halo_copies:
            copy.start()
    gate_copy.wait()
    rows, cols = cumulative(gate_ref[...])
    for j in range(HALF):
        if j % STEP == 0:
            for copy in copies[j // STEP]:
                copy.wait()
        at = slice(j * DH, (j + 1) * DH)
        last = rows[j : j + 1, DH - 1 : DH]
        head = jnp.exp(cols[:, j : j + 1])
        tail = jnp.exp(last - cols[:, j : j + 1])
        kt = (k_ref[:, at].astype(F32) * tail).astype(BF16)
        qh = (q_ref[:, at].astype(F32) * head).astype(BF16)
        s = dot(kt, v_ref[:, at], 0, 0).astype(BF16)
        g = dot(qh, g_ref[:, at], 0, 0).astype(BF16)
        d = decay_tile(jnp.exp(last))
        for r in range(2):
            part = slice(r * 64, (r + 1) * 64)
            msg_ref[2 * j + r, 0:64, :] = s[part]
            msg_ref[2 * j + r, 64:128, :] = g[part]
            msg_ref[2 * j + r, 128:144, :] = d
    if with_halo:
        for copy in halo_copies:
            copy.wait()


def combine_kernel(c_ref, own_ref, other_ref, out_ref, kept_ref):
    kept_ref[...] = other_ref[...]
    first = c_ref[0] == 0

    def body(a_ref, b_ref):
        for p in range(PLANE):
            da = decay_of(a_ref[p, 128:144, :])
            db = decay_of(b_ref[p, 128:144, :])
            out_ref[p, 0:64, :] = (db * a_ref[p, 0:64, :].astype(F32) + b_ref[p, 0:64, :].astype(F32)).astype(BF16)
            out_ref[p, 64:128, :] = (a_ref[p, 64:128, :].astype(F32) + da * b_ref[p, 64:128, :].astype(F32)).astype(BF16)
            out_ref[p, 128:144, :] = decay_tile(da * db)

    @pl.when(first)
    def _():
        body(own_ref, other_ref)

    @pl.when(jnp.logical_not(first))
    def _():
        body(other_ref, own_ref)


def plane_kernel(z_ref, msg_ref, out_ref):
    fwd = jnp.zeros((64, DH), F32)
    bwd = jnp.zeros((64, DH), F32)
    d = jnp.ones((1, DH), F32)
    for p in range(PLANE):
        b = PLANE - 1 - p
        dp = decay_of(msg_ref[p, 128:144, :])
        fwd = dp * fwd + msg_ref[p, 0:64, :].astype(F32)
        bwd = decay_of(msg_ref[b, 128:144, :]) * bwd + msg_ref[b, 64:128, :].astype(F32)
        d = d * dp
    tile = decay_tile(d)
    for i in range(GRID[0]):
        out_ref[i, 0:64, :] = jnp.where(i > z_ref[0], fwd, bwd).astype(BF16)
        out_ref[i, 64:80, :] = tile


def incoming_kernel(z_ref, msg_ref, planes_ref, out_ref):
    z = z_ref[0]
    n = GRID[0]
    fwd = jnp.zeros((64, DH), F32)
    bwd = jnp.zeros((64, DH), F32)
    for i in range(n):
        b = n - 1 - i
        new_f = decay_of(planes_ref[i, 64:80, :]) * fwd + planes_ref[i, 0:64, :].astype(F32)
        fwd = jnp.where(i < z, new_f, fwd)
        new_b = decay_of(planes_ref[b, 64:80, :]) * bwd + planes_ref[b, 0:64, :].astype(F32)
        bwd = jnp.where(b > z, new_b, bwd)
    for p in range(PLANE):
        b = PLANE - 1 - p
        out_ref[p, 0:64, :] = fwd.astype(BF16)
        out_ref[b, 64:128, :] = bwd.astype(BF16)
        fwd = decay_of(msg_ref[p, 128:144, :]) * fwd + msg_ref[p, 0:64, :].astype(F32)
        bwd = decay_of(msg_ref[b, 128:144, :]) * bwd + msg_ref[b, 64:128, :].astype(F32)


def hand_kernel(c_ref, chip_ref, own_ref, other_ref, mine_ref, theirs_ref):
    first = c_ref[0] == 0

    def body(is_first):
        for p in range(PLANE):
            fwd = chip_ref[p, 0:64, :]
            bwd = chip_ref[p, 64:128, :]
            inner = own_ref if is_first else other_ref
            outer = other_ref if is_first else own_ref
            late_f = (decay_of(inner[p, 128:144, :]) * fwd.astype(F32) + inner[p, 0:64, :].astype(F32)).astype(BF16)
            early_b = (decay_of(outer[p, 128:144, :]) * bwd.astype(F32) + outer[p, 64:128, :].astype(F32)).astype(BF16)
            early_ref = mine_ref if is_first else theirs_ref
            late_ref = theirs_ref if is_first else mine_ref
            early_ref[p, 0:64, :] = fwd
            early_ref[p, 64:128, :] = early_b
            late_ref[p, 0:64, :] = late_f
            late_ref[p, 64:128, :] = bwd

    @pl.when(first)
    def _():
        body(True)

    @pl.when(jnp.logical_not(first))
    def _():
        body(False)


def window_kernel(lin_scale, live_ref, q_hbm, k_hbm, v_hbm, g_hbm, halo_ref, gate_hbm, *rest):
    outs, row_ref = rest[:5], rest[5]
    q_ref, k_ref, v_ref, g_ref, *stages, gate_ref, sems, out_sems, gate_sem = rest[6:]
    o_ref, qg_ref, kg_ref, vg_ref, back_ref = stages
    gate_copy = pltpu.make_async_copy(gate_hbm, gate_ref, gate_sem)
    gate_copy.start()
    width = WSTEP * DH

    def copies(i):
        at = pl.ds(pl.multiple_of(i * width, width), width)
        return [
            pltpu.make_async_copy(big.at[:, at], small.at[:, at], sems.at[i, n])
            for n, (big, small) in enumerate(((q_hbm, q_ref), (k_hbm, k_ref), (v_hbm, v_ref), (g_hbm, g_ref)))
        ]

    def out_copies(i):
        at = pl.ds(pl.multiple_of(i * width, width), width)
        return [pltpu.make_async_copy(stage.at[:, at], out.at[:, at], out_sems.at[i, n]) for n, (stage, out) in enumerate(zip(stages, outs, strict=True))]

    for i in range(16 // WSTEP):
        for copy in copies(i):
            copy.start()
    live = live_ref[0] > 0
    t = lax.broadcasted_iota(jnp.int32, (DH, DH), 0)
    lane = lax.broadcasted_iota(jnp.int32, (DH, DH), 1)
    key = jnp.where(t < W, lane - W, lane)
    causal = (key >= 0) & (key <= t)
    banded = (key > t - W) & (key <= t) & ((key >= 0) | live)
    scale = DH**-0.5
    lin_bias = jnp.where(causal, math.log(lin_scale), -jnp.inf)
    win_bias = jnp.where(banded, 0.0, -jnp.inf)
    gate_copy.wait()
    row_ref[...] = cumulative(gate_ref[...])[0]

    def step(i, carry):
        for copy in copies(i):
            copy.wait()
        for j in range(WSTEP):
            at = pl.ds(pl.multiple_of(i * width + j * DH, DH), DH)
            q, k, v, g = q_ref[:, at], k_ref[:, at], v_ref[:, at], g_ref[:, at]
            kx = jnp.concatenate([halo_ref[0:W, at], k[0:W]], axis=0)
            vx = jnp.concatenate([halo_ref[W : 2 * W, at], v[0:W]], axis=0)
            a = jnp.concatenate([dot(q[0:W], kx, 1, 1), dot(q[W:], k, 1, 1)], axis=0)
            b = jnp.concatenate([dot(g[0:W], vx, 1, 1), dot(g[W:], v, 1, 1)], axis=0)
            row = jnp.broadcast_to(row_ref[pl.ds(i * WSTEP + j, 1), :], (DH, DH))
            shifted = jnp.concatenate([row[:W, W:], row[:W, :W]], axis=1)
            gap = row.T - jnp.concatenate([shifted, row[W:]], axis=0)
            decay = jnp.exp(gap + lin_bias)
            logits = a * scale + win_bias
            e = jnp.exp(logits - jnp.max(logits, axis=1, keepdims=True))
            inv = 1.0 / jnp.sum(e, axis=1, keepdims=True)
            delta = jnp.sum(e * b, axis=1, keepdims=True) * inv
            w1 = (e * inv + decay * a).astype(BF16)
            w2 = (e * (inv * scale) * (b - delta) + decay * b).astype(BF16)
            o_ref[0:W, at] = dot(w1[0:W], vx, 1, 0)
            o_ref[W:, at] = dot(w1[W:], v, 1, 0)
            qg_ref[0:W, at] = dot(w2[0:W], kx, 1, 0)
            qg_ref[W:, at] = dot(w2[W:], k, 1, 0)
            k_top = dot(w2[0:W], q[0:W], 0, 0)
            k_low = dot(w2[W:], q[W:], 0, 0)
            v_top = dot(w1[0:W], g[0:W], 0, 0)
            v_low = dot(w1[W:], g[W:], 0, 0)
            kg_ref[0:W, at] = k_low[0:W] + k_top[W:]
            kg_ref[W:, at] = k_low[W:]
            vg_ref[0:W, at] = v_low[0:W] + v_top[W:]
            vg_ref[W:, at] = v_low[W:]
            back_ref[0:W, at] = k_top[0:W].astype(BF16)
            back_ref[W : 2 * W, at] = v_top[0:W].astype(BF16)
        for copy in out_copies(i):
            copy.start()
        return carry

    lax.fori_loop(0, 16 // WSTEP, step, 0)
    for i in range(16 // WSTEP):
        for copy in out_copies(i):
            copy.wait()


def final_kernel(lin_scale, n_alias, sel_ref, q_ref, k_ref, v_ref, g_ref, ret_hbm, row_ref, st_ref, po_ref, pq_ref, pk_ref, pv_ref, *rest):
    outs = rest[n_alias : n_alias + 4]
    stage_ref, ret_ref, sems, ret_sem = rest[n_alias + 4 :]
    sel = sel_ref[0]
    ret_copy = pltpu.make_async_copy(ret_hbm.at[:, pl.ds(pl.multiple_of(sel * COLS, COLS), COLS)], ret_ref, ret_sem)
    ret_copy.start()
    rows = row_ref[pl.ds(pl.multiple_of(sel * HALF, HALF), HALF), :]
    heads = jnp.exp(rows).T * lin_scale
    tails = jnp.exp(rows[:, DH - 1 :] - rows).T * lin_scale
    width = STEP * DH
    copies = []

    def send(n, j):
        if j % STEP == STEP - 1:
            i = j // STEP
            target = pl.ds(pl.multiple_of(sel * COLS + i * width, width), width)
            copy = pltpu.make_async_copy(stage_ref.at[n, :, i * width : (i + 1) * width], outs[n].at[:, target], sems.at[i, n])
            copy.start()
            copies.append(copy)

    for j in range(HALF):
        at = pl.ds(pl.multiple_of(sel * COLS + j * DH, DH), DH)
        to = slice(j * DH, (j + 1) * DH)
        head = heads[:, j : j + 1]
        s = jnp.concatenate([st_ref[2 * j, 0:64, :], st_ref[2 * j + 1, 0:64, :]], axis=0)
        stage_ref[0, :, to] = (po_ref[:, at] + head * dot(q_ref[:, at], s, 1, 0)).astype(BF16)
        stage_ref[1, :, to] = (pq_ref[:, at] + head * dot(g_ref[:, at], s, 1, 1)).astype(BF16)
        send(0, j)
        send(1, j)
    ret_copy.wait()
    for j in range(HALF):
        at = pl.ds(pl.multiple_of(sel * COLS + j * DH, DH), DH)
        to = slice(j * DH, (j + 1) * DH)
        tail = tails[:, j : j + 1]
        m = jnp.concatenate([st_ref[2 * j, 64:128, :], st_ref[2 * j + 1, 64:128, :]], axis=0)
        kg = pk_ref[:, at] + tail * dot(v_ref[:, at], m, 1, 1)
        vg = pv_ref[:, at] + tail * dot(k_ref[:, at], m, 1, 0)
        stage_ref[2, 0:W, to] = kg[0:W].astype(BF16)
        stage_ref[2, W:, to] = (kg[W:] + ret_ref[0:W, to].astype(F32)).astype(BF16)
        stage_ref[3, 0:W, to] = vg[0:W].astype(BF16)
        stage_ref[3, W:, to] = (vg[W:] + ret_ref[W : 2 * W, to].astype(F32)).astype(BF16)
        send(2, j)
        send(3, j)
    for copy in copies:
        copy.wait()


def vmem(mib):
    return pltpu.CompilerParams(vmem_limit_bytes=mib << 20)


def cost(flops, nbytes):
    return pl.CostEstimate(flops=int(flops), bytes_accessed=int(nbytes), transcendentals=0)


IN_VMEM = pl.BlockSpec(memory_space=pltpu.VMEM)
IN_HBM = pl.BlockSpec(memory_space=pltpu.HBM)
IN_SMEM = pl.BlockSpec(memory_space=pltpu.SMEM)
DMA = pltpu.SemaphoreType.DMA


def local_states(sel, q, k, v, g, gates, with_halo):
    outs = [pltpu.VMEM((PLANE, MSG, DH), BF16)]
    sems = [DMA((HALF // STEP, 4)), DMA]
    if with_halo:
        outs.append(pltpu.VMEM((2 * W, 2048), BF16))
        sems.append(DMA((2,)))
    return pl.pallas_call(
        lambda *refs: states_kernel(with_halo, *refs),
        out_shape=tuple(outs),
        in_specs=[IN_SMEM] + [IN_HBM] * 5,
        out_specs=(IN_VMEM,) * len(outs),
        scratch_shapes=[pltpu.VMEM((128, COLS), BF16)] * 4 + [pltpu.VMEM((HALF, DH), F32)] + sems,
        cost_estimate=cost(7e7, 1.6e6),
        compiler_params=vmem(8),
        name="local_states",
    )(sel, q, k, v, g, gates)


def small_call(body, scalar, arrays, outs):
    return pl.pallas_call(
        body,
        out_shape=tuple(pltpu.VMEM(s, BF16) for s in outs),
        in_specs=[IN_SMEM] + [IN_VMEM] * len(arrays),
        out_specs=(IN_VMEM,) * len(outs),
        cost_estimate=cost(1e6, 2e6),
        compiler_params=vmem(4),
    )(scalar, *arrays)


def window(lin_scale, live, q, k, v, g, halo, gates):
    full = (128, 2048)
    steps = 16 // WSTEP
    return pl.pallas_call(
        lambda *refs: window_kernel(lin_scale, *refs),
        out_shape=tuple(pltpu.HBM(full, F32) for _ in range(4)) + (pltpu.HBM(full, BF16), pltpu.VMEM((16, DH), F32)),
        in_specs=[IN_SMEM] + [IN_HBM] * 4 + [IN_VMEM, IN_HBM],
        out_specs=(IN_HBM,) * 5 + (IN_VMEM,),
        scratch_shapes=[pltpu.VMEM(full, BF16)] * 4
        + [pltpu.VMEM(full, F32)] * 4
        + [pltpu.VMEM(full, BF16), pltpu.VMEM((16, DH), F32), DMA((steps, 4)), DMA((steps, 5)), DMA],
        cost_estimate=cost(6e8, 8e6),
        compiler_params=vmem(14),
        name="window",
    )(live, q, k, v, g, halo, gates)


def finish(lin_scale, sel, q, k, v, g, ret, rows, states, parts, previous):
    n = len(previous)
    return pl.pallas_call(
        lambda *refs: final_kernel(lin_scale, n, *refs),
        out_shape=tuple(pltpu.HBM((128, 2048), BF16) for _ in range(4)),
        in_specs=[IN_SMEM] + [IN_VMEM] * 4 + [IN_HBM] + [IN_VMEM] * 6 + [IN_HBM] * n,
        out_specs=(IN_HBM,) * 4,
        scratch_shapes=[pltpu.VMEM((4, 128, COLS), BF16), pltpu.VMEM((128, COLS), BF16), DMA((HALF // STEP, 4)), DMA],
        input_output_aliases={12 + i: i for i in range(n)},
        cost_estimate=cost(3e8, 5e6),
        compiler_params=vmem(8),
        name="finish",
    )(sel, q, k, v, g, ret, rows, states, *parts, *previous)


def per_device(q, k, v, g, gates):
    lin_scale = (DH * q.shape[0] * 256) ** (-0.5)
    core = lax.axis_index("c")
    mine = core[None].astype(jnp.int32)
    theirs = 1 - mine
    z = lax.axis_index("z")[None].astype(jnp.int32)
    live = (lax.axis_index(AXES) > 0)[None].astype(jnp.int32)
    swap = [(0, 1), (1, 0)]
    late = (q, k, v, g)
    q, k, v, g, gates = (pltpu.with_memory_space_constraint(a, pltpu.HBM) for a in (q, k, v, g, gates))

    sent, edge = local_states(theirs, q, k, v, g, gates, True)
    other = lax.ppermute(sent, "c", swap)
    halo = lax.ppermute(edge, AXES, [(i, i + 1) for i in range(255)])
    (own,) = local_states(mine, q, k, v, g, gates, False)
    chip, other = small_call(combine_kernel, mine, (own, other), [(PLANE, MSG, DH)] * 2)
    plane = lax.all_to_all(chip, ("x", "y"), 0, 0, tiled=True)
    *parts, back, sums = window(lin_scale, live, q, k, v, g, halo, gates)
    (total,) = small_call(plane_kernel, z, (plane,), [(GRID[0], 80, DH)])
    planes = lax.all_to_all(total, "z", 0, 0, tiled=True)
    ret = lax.ppermute(back, AXES, [(i + 1, i) for i in range(255)])
    (incoming,) = small_call(incoming_kernel, z, (plane, planes), [(PLANE, DH, DH)])
    chip_in = lax.all_to_all(incoming, ("x", "y"), 0, 0, tiled=True)
    st_mine, st_theirs = small_call(hand_kernel, mine, (chip_in, own, other), [(PLANE, DH, DH)] * 2)
    st_other = lax.ppermute(st_theirs, "c", swap)
    outs = finish(lin_scale, mine, *late, ret, sums, st_mine, parts, ())
    return finish(lin_scale, theirs, *late, ret, sums, st_other, parts, outs)


def solution(mesh):
    fine = Mesh(mesh.devices.reshape(GRID), AXES)
    rows = P(AXES, None)

    return jax.shard_map(
        per_device,
        mesh=fine,
        in_specs=(rows,) * 4 + (P(None, AXES),),
        out_specs=(rows,) * 4,
        check_vma=False,
    )
```

time: 95.8 us -> 86.1 us (0.90)
  the two profiles are of different devices: /device:TPU:31 before, /device:TPU:127 now
where the time goes in v2:
time: 86.1 us; the launch traced here: 85.4 us
  starting transfers between devices  32.7 us (38%)
  Pallas kernels  24.7 us (29%)
  waiting for transfers between devices  22.2 us (26%)
  local copies, waits for them, and re-layouts  4.92 us (6%)
    ppermute x1, waiting for transfers between devices, per_device(): ret = lax.ppermute(back, AXES, [(i + 1, i) for i in range(255)])  13.8 us
    pallas_call x1, Pallas kernels, window(): pl.pallas_call(lambda *refs: window_kernel(lin_scale, *refs), out_shape=t...  10.9 us
    ppermute x1, starting transfers between devices, per_device(): halo = lax.ppermute(edge, AXES, [(i, i + 1) for i in range(255)])  9.3 us
    all_to_all x1, waiting for transfers between devices, per_device(): plane = lax.all_to_all(chip, ('x', 'y'), 0, 0, tiled=True)  8.41 us
    pallas_call x2, Pallas kernels, local_states(): pl.pallas_call(lambda *refs: states_kernel(with_halo, *refs), out_shape=t...  7.14 us
    all_to_all x1, starting transfers between devices, per_device(): planes = lax.all_to_all(total, 'z', 0, 0, tiled=True)  7.1 us
    all_to_all x1, starting transfers between devices, per_device(): plane = lax.all_to_all(chip, ('x', 'y'), 0, 0, tiled=True)  6.53 us
    all_to_all x1, starting transfers between devices, per_device(): chip_in = lax.all_to_all(incoming, ('x', 'y'), 0, 0, tiled=True)  6.08 us
  transfers between devices with their start and end apart: 7, of which 2 were waited for; matrix products, arithmetic and copies ran while one was open for 0% of the time, Pallas kernels for 20%

profile of v2, /device:TPU:127, one launch (start us, length us, event | category | flops | bytes accessed | tf_op | source)
XLA Modules:
  0.0 85.4 jit_solution(15719603383561360641)
XLA Ops:
  0.6 4.0 %local_states.2 = (bf16[16,144,128]{2,1,0:T(8,128)(2,1)S(1)}, bf16[128,2048]{1,0:T(8,128)(2,1)}) custom-call(s32[1]{0:T(128)S(6)} %sub.3.refs_0_, bf16[128,2048]{1,0:T(8,128)(2,1)} %refs_1_.9, bf16[128,2048]{1,0:T(8,128)(2,1)} %refs_2_.9, bf16[128,2048]{1,0:T(8,128)(2,1)} %refs_3_.9, bf16[128,2048]{1,0:T(8,128)(2,1)} %refs_4_.9, f32[16,128]{1,0:T(8,128)} %refs_5_.3), custom_call_target="tpu_custom_call" | custom-call | flops 70000000 | bytes 1600000 | tf_op jit(solution)/shard_map/local_states/pallas_call | solution.py:332
  4.7 0.8 collective-permute-start.2
  5.4 3.1 %local_states.3.own_ref = bf16[16,144,128]{2,1,0:T(8,128)(2,1)S(1)} custom-call(s32[1]{0:T(128)} %bitcast.refs_0_.c_ref, bf16[128,2048]{1,0:T(8,128)(2,1)} %refs_1_.9, bf16[128,2048]{1,0:T(8,128)(2,1)} %refs_2_.9, bf16[128,2048]{1,0:T(8,128)(2,1)} %refs_3_.9, bf16[128,2048]{1,0:T(8,128)(2,1)} %refs_4_.9, f32[16,128]{1,0:T(8,128)} %refs_5_.3), custom_call_target="tpu_custom_call" | custom-call | flops 70000000 | bytes 1600000 | tf_op jit(solution)/shard_map/local_states/pallas_call | solution.py:332
  8.6 1.1 %shard_map.84 = (bf16[16,144,128]{2,1,0:T(8,128)(2,1)}, bf16[16,144,128]{2,1,0:T(8,128)(2,1)S(1)}) custom-call(s32[1]{0:T(128)} %bitcast.refs_0_.c_ref, bf16[16,144,128]{2,1,0:T(8,128)(2,1)S(1)} %local_states.3.own_ref, bf16[16,144,128]{2,1,0:T(8,128)(2,1)S(1)} %collective-permute-done.2.other_ref), custom_call_target="tpu_custom_call" | custom-call | flops 1000000 | bytes 2000000 | tf_op jit(solution)/shard_map/pallas_call | solution.py:345
  9.6 6.5 %all-to-all-start = ((bf16[16,144,128]{2,1,0:T(8,128)(2,1)}), bf16[16,144,128]{2,1,0:T(8,128)(2,1)S(1)}, u32[]{:S(2)}, u32[]{:S(2)}) async-start(bf16[16,144,128]{2,1,0:T(8,128)(2,1)} %get-tuple-element.24), calls=%async_computation | async-start | bytes 1179648 | tf_op jit(solution)/shard_map/all_to_all | solution.py:403
  16.2 8.4 %all-to-all-done.msg_ref = bf16[16,144,128]{2,1,0:T(8,128)(2,1)S(1)} async-done(((bf16[16,144,128]{2,1,0:T(8,128)(2,1)}), bf16[16,144,128]{2,1,0:T(8,128)(2,1)S(1)}, u32[]{:S(2)}, u32[]{:S(2)}) %all-to-all-start) | async-done | bytes 589856 | tf_op jit(solution)/shard_map/all_to_all | solution.py:403
  24.6 0.8 shard_map.85
  25.4 7.1 %all-to-all-start.1 = ((bf16[8,80,128]{2,1,0:T(8,128)(2,1)}), bf16[8,80,128]{2,1,0:T(8,128)(2,1)S(1)}, u32[]{:S(2)}, u32[]{:S(2)}) async-start(bf16[8,80,128]{2,1,0:T(8,128)(2,1)} %shard_map.85), calls=%async_computation.1 | async-start | bytes 327680 | tf_op jit(solution)/shard_map/all_to_all | solution.py:406
  32.5 9.3 %collective-permute-start = (bf16[128,2048]{1,0:T(8,128)(2,1)}, bf16[128,2048]{1,0:T(8,128)(2,1)S(1)}, u32[]{:S(2)}, u32[]{:S(2)}) collective-permute-start(bf16[128,2048]{1,0:T(8,128)(2,1)} %get-tuple-element.20), channel_id=1, source_target_pairs={{0,1},{1,2},{2,3},{3,4},{4,5},{5,6},{6,7},{7,8},{8,9},{9,10},{10,1... | collective-permute-start | bytes 1572872 | tf_op jit(solution)/shard_map/ppermute | solution.py:400
  41.8 1.0 %shard_map.86 = bf16[16,128,128]{2,1,0:T(8,128)(2,1)} custom-call(s32[1]{0:T(128)} %bitcast.2.z_ref, bf16[16,144,128]{2,1,0:T(8,128)(2,1)S(1)} %all-to-all-done.msg_ref, bf16[8,80,128]{2,1,0:T(8,128)(2,1)S(1)} %all-to-all-done.1.planes_ref), custom_call_target="tpu_custom_call" | custom-call | flops 1000000 | bytes 2000000 | tf_op jit(solution)/shard_map/pallas_call | solution.py:345
  42.8 6.1 %all-to-all-start.2 = ((bf16[16,128,128]{2,1,0:T(8,128)(2,1)}), bf16[16,128,128]{2,1,0:T(8,128)(2,1)S(1)}, u32[]{:S(2)}, u32[]{:S(2)}) async-start(bf16[16,128,128]{2,1,0:T(8,128)(2,1)} %shard_map.86), calls=%async_computation.2 | async-start | bytes 1048576 | tf_op jit(solution)/shard_map/all_to_all | solution.py:409
  48.9 0.0 copy-start.3
  48.9 10.9 %window.1 = (f32[128,2048]{1,0:T(8,128)}, f32[128,2048]{1,0:T(8,128)}, f32[128,2048]{1,0:T(8,128)}, f32[128,2048]{1,0:T(8,128)}, bf16[128,2048]{1,0:T(8,128)(2,1)}, /*index=5*/f32[16,128]{1,0:T(8,128)S(1)}) custom-call(s32[1]{0:T(128)} %bitcast.1.refs_0_, bf16[128,2048]{1,0:T(8,128)(2,1)} %refs_1_.9, bf16[128,2048]{1,0:T(8,128)(2,1)} %refs_2_.9, ...), custom_call_target="tpu_custom_call" | custom-call | flops 600000000 | bytes 8000000 | tf_op jit(solution)/shard_map/window/pallas_call | solution.py:358
  59.8 1.9 %collective-permute-start.1 = (bf16[128,2048]{1,0:T(8,128)(2,1)}, bf16[128,2048]{1,0:T(8,128)(2,1)S(1)}, u32[]{:S(2)}, u32[]{:S(2)}) collective-permute-start(bf16[128,2048]{1,0:T(8,128)(2,1)} %get-tuple-element.21), channel_id=1, source_target_pairs={{1,0},{2,1},{3,2},{4,3},{5,4},{6,5},{7,6},{8,7},{9,8},{10,9},{11,1... | collective-permute-start | bytes 1572872 | tf_op jit(solution)/shard_map/ppermute | solution.py:407
  61.8 0.0 copy-start.2
  61.8 0.2 shard_map.87
  62.0 1.0 %collective-permute-start.3 = (bf16[16,128,128]{2,1,0:T(8,128)(2,1)S(1)}, bf16[16,128,128]{2,1,0:T(8,128)(2,1)S(1)}, u32[]{:S(2)}, u32[]{:S(2)}) collective-permute-start(bf16[16,128,128]{2,1,0:T(8,128)(2,1)S(1)} %get-tuple-element.26), channel_id=1, source_target_pairs={{0,1},{1,0},{2,3},{3,2},{4,5},{5,4},{6,7},{7,6},{8,9},{9,8},{10,11... | collective-permute-start | bytes 1572872 | tf_op jit(solution)/shard_map/ppermute | solution.py:411
  63.1 13.8 %collective-permute-done.1.refs_5_ = bf16[128,2048]{1,0:T(8,128)(2,1)S(1)} collective-permute-done((bf16[128,2048]{1,0:T(8,128)(2,1)}, bf16[128,2048]{1,0:T(8,128)(2,1)S(1)}, u32[]{:S(2)}, u32[]{:S(2)}) %collective-permute-start.1) | collective-permute-done | bytes 524320 | tf_op jit(solution)/shard_map/ppermute | solution.py:407
  76.9 1.2 %copy-done.4 = f32[128,2048]{1,0:T(8,128)S(1)} copy-done((f32[128,2048]{1,0:T(8,128)S(1)}, f32[128,2048]{1,0:T(8,128)}, u32[]{:S(2)}) %copy-start.4) | copy-done | bytes 1048600
  78.1 1.2 %copy-done.5 = f32[128,2048]{1,0:T(8,128)S(1)} copy-done((f32[128,2048]{1,0:T(8,128)S(1)}, f32[128,2048]{1,0:T(8,128)}, u32[]{:S(2)}) %copy-start.5) | copy-done | bytes 1048600
  79.3 1.2 %copy-done.6 = f32[128,2048]{1,0:T(8,128)S(1)} copy-done((f32[128,2048]{1,0:T(8,128)S(1)}, f32[128,2048]{1,0:T(8,128)}, u32[]{:S(2)}) %copy-start.6) | copy-done | bytes 1048600
  80.6 1.2 %copy-done.7 = f32[128,2048]{1,0:T(8,128)S(1)} copy-done((f32[128,2048]{1,0:T(8,128)S(1)}, f32[128,2048]{1,0:T(8,128)}, u32[]{:S(2)}) %copy-start.7) | copy-done | bytes 1048600
  81.8 1.8 %finish.2 = (bf16[128,2048]{1,0:T(8,128)(2,1)}, bf16[128,2048]{1,0:T(8,128)(2,1)}, bf16[128,2048]{1,0:T(8,128)(2,1)}, bf16[128,2048]{1,0:T(8,128)(2,1)}) custom-call(s32[1]{0:T(128)} %bitcast.refs_0_.c_ref, bf16[128,2048]{1,0:T(8,128)(2,1)S(1)} %copy-done, bf16[128,2048]{1,0:T(8,128)(2,1)S(1)} %copy-done.1, bf16[128,2048]{1,0:T(8,128)(2,1)S(1)} %copy-done.2, ...), custom_call_target="tpu_custom_call" | custom-call | flops 300000000 | bytes 5000000 | tf_op jit(solution)/shard_map/finish/pallas_call | solution.py:374
  83.6 1.8 %finish.3 = (bf16[128,2048]{1,0:T(8,128)(2,1)}, bf16[128,2048]{1,0:T(8,128)(2,1)}, bf16[128,2048]{1,0:T(8,128)(2,1)}, bf16[128,2048]{1,0:T(8,128)(2,1)}) custom-call(s32[1]{0:T(128)S(6)} %sub.3.refs_0_, bf16[128,2048]{1,0:T(8,128)(2,1)S(1)} %copy-done, ...), custom_call_target="tpu_custom_call", output_to_operand_aliasing={{0}: (12, {}), {1}: (13, {}), {2}: (14, {}), {3}: (15, {})} | custom-call | flops 300000000 | bytes 5000000 | tf_op jit(solution)/shard_map/finish/pallas_call | solution.py:374
  (15 shorter events, 0.0 us)
Async XLA Ops:
  4.7 3.9 %collective-permute-start.2 = (bf16[16,144,128]{2,1,0:T(8,128)(2,1)S(1)}, bf16[16,144,128]{2,1,0:T(8,128)(2,1)S(1)}, u32[]{:S(2)}, u32[]{:S(2)}) collective-permute-start(bf16[16,144,128]{2,1,0:T(8,128)(2,1)S(1)} %get-tuple-element.23), channel_id=1, source_target_pairs={{0,1},{1,0},{2,3},{3,2},{4,5},{5,4},{6,7},{7,6},{8,9},{9,8},{10,11... | collective-permute-start | bytes 1769480 | tf_op jit(solution)/shard_map/ppermute | solution.py:399
  9.6 14.9 %all-to-all-start = ((bf16[16,144,128]{2,1,0:T(8,128)(2,1)}), bf16[16,144,128]{2,1,0:T(8,128)(2,1)S(1)}, u32[]{:S(2)}, u32[]{:S(2)}) async-start(bf16[16,144,128]{2,1,0:T(8,128)(2,1)} %get-tuple-element.24), calls=%async_computation | async-start | bytes 1179648 | tf_op jit(solution)/shard_map/all_to_all | solution.py:403
  25.4 16.4 %all-to-all-start.1 = ((bf16[8,80,128]{2,1,0:T(8,128)(2,1)}), bf16[8,80,128]{2,1,0:T(8,128)(2,1)S(1)}, u32[]{:S(2)}, u32[]{:S(2)}) async-start(bf16[8,80,128]{2,1,0:T(8,128)(2,1)} %shard_map.85), calls=%async_computation.1 | async-start | bytes 327680 | tf_op jit(solution)/shard_map/all_to_all | solution.py:406
  32.5 16.4 %collective-permute-start = (bf16[128,2048]{1,0:T(8,128)(2,1)}, bf16[128,2048]{1,0:T(8,128)(2,1)S(1)}, u32[]{:S(2)}, u32[]{:S(2)}) collective-permute-start(bf16[128,2048]{1,0:T(8,128)(2,1)} %get-tuple-element.20), channel_id=1, source_target_pairs={{0,1},{1,2},{2,3},{3,4},{4,5},{5,6},{6,7},{7,8},{8,9},{9,10},{10,1... | collective-permute-start | bytes 1572872 | tf_op jit(solution)/shard_map/ppermute | solution.py:400
  42.8 18.9 %all-to-all-start.2 = ((bf16[16,128,128]{2,1,0:T(8,128)(2,1)}), bf16[16,128,128]{2,1,0:T(8,128)(2,1)S(1)}, u32[]{:S(2)}, u32[]{:S(2)}) async-start(bf16[16,128,128]{2,1,0:T(8,128)(2,1)} %shard_map.86), calls=%async_computation.2 | async-start | bytes 1048576 | tf_op jit(solution)/shard_map/all_to_all | solution.py:409
  48.9 27.9 %copy-start.3 = (bf16[128,2048]{1,0:T(8,128)(2,1)S(1)}, bf16[128,2048]{1,0:T(8,128)(2,1)}, u32[]{:S(2)}) copy-start(bf16[128,2048]{1,0:T(8,128)(2,1)} %refs_4_.9) | copy-start | bytes 1572868
  59.8 17.1 %collective-permute-start.1 = (bf16[128,2048]{1,0:T(8,128)(2,1)}, bf16[128,2048]{1,0:T(8,128)(2,1)S(1)}, u32[]{:S(2)}, u32[]{:S(2)}) collective-permute-start(bf16[128,2048]{1,0:T(8,128)(2,1)} %get-tuple-element.21), channel_id=1, source_target_pairs={{1,0},{2,1},{3,2},{4,3},{5,4},{6,5},{7,6},{8,7},{9,8},{10,9},{11,1... | collective-permute-start | bytes 1572872 | tf_op jit(solution)/shard_map/ppermute | solution.py:407
  61.7 15.1 %copy-start = (bf16[128,2048]{1,0:T(8,128)(2,1)S(1)}, bf16[128,2048]{1,0:T(8,128)(2,1)}, u32[]{:S(2)}) copy-start(bf16[128,2048]{1,0:T(8,128)(2,1)} %refs_1_.9) | copy-start | bytes 1572868
  61.8 15.1 %copy-start.1 = (bf16[128,2048]{1,0:T(8,128)(2,1)S(1)}, bf16[128,2048]{1,0:T(8,128)(2,1)}, u32[]{:S(2)}) copy-start(bf16[128,2048]{1,0:T(8,128)(2,1)} %refs_2_.9) | copy-start | bytes 1572868
  61.8 15.1 %copy-start.2 = (bf16[128,2048]{1,0:T(8,128)(2,1)S(1)}, bf16[128,2048]{1,0:T(8,128)(2,1)}, u32[]{:S(2)}) copy-start(bf16[128,2048]{1,0:T(8,128)(2,1)} %refs_3_.9) | copy-start | bytes 1572868
  62.0 21.5 %collective-permute-start.3 = (bf16[16,128,128]{2,1,0:T(8,128)(2,1)S(1)}, bf16[16,128,128]{2,1,0:T(8,128)(2,1)S(1)}, u32[]{:S(2)}, u32[]{:S(2)}) collective-permute-start(bf16[16,128,128]{2,1,0:T(8,128)(2,1)S(1)} %get-tuple-element.26), channel_id=1, source_target_pairs={{0,1},{1,0},{2,3},{3,2},{4,5},{5,4},{6,7},{7,6},{8,9},{9,8},{10,11... | collective-permute-start | bytes 1572872 | tf_op jit(solution)/shard_map/ppermute | solution.py:411
  76.9 1.2 %copy-start.4 = (f32[128,2048]{1,0:T(8,128)S(1)}, f32[128,2048]{1,0:T(8,128)}, u32[]{:S(2)}) copy-start(f32[128,2048]{1,0:T(8,128)} %get-tuple-element.27.refs_8_) | copy-start | bytes 3145732
  78.1 1.2 %copy-start.5 = (f32[128,2048]{1,0:T(8,128)S(1)}, f32[128,2048]{1,0:T(8,128)}, u32[]{:S(2)}) copy-start(f32[128,2048]{1,0:T(8,128)} %get-tuple-element.28.refs_9_) | copy-start | bytes 3145732
  79.3 1.2 %copy-start.6 = (f32[128,2048]{1,0:T(8,128)S(1)}, f32[128,2048]{1,0:T(8,128)}, u32[]{:S(2)}) copy-start(f32[128,2048]{1,0:T(8,128)} %get-tuple-element.29.refs_10_) | copy-start | bytes 3145732
  80.6 1.2 %copy-start.7 = (f32[128,2048]{1,0:T(8,128)S(1)}, f32[128,2048]{1,0:T(8,128)}, u32[]{:S(2)}) copy-start(f32[128,2048]{1,0:T(8,128)} %get-tuple-element.30.refs_11_) | copy-start | bytes 3145732

commit v3 on v2

--- a/solution.py
+++ b/solution.py
@@ -16,8 +16,10 @@
 DH = 128
 HALF = 8
 COLS = HALF * DH
-STEP = 2
-WSTEP = 4
+STEP = 8
+OSTEP = 2
+WSTEP = 16
+GROUP = 8
 MSG = 144
 F32 = jnp.float32
 BF16 = jnp.bfloat16
@@ -32,8 +34,7 @@
     i = lax.broadcasted_iota(jnp.int32, (n, n), 0)
     j = lax.broadcasted_iota(jnp.int32, (n, n), 1)
     upper = (i <= j).astype(F32)
-    rows = lax.dot_general(gates, upper, (((1,), (0,)), ((), ())), precision=lax.Precision.HIGHEST, preferred_element_type=F32)
-    return rows, rows.T
+    return lax.dot_general(gates, upper, (((1,), (0,)), ((), ())), precision=lax.Precision.HIGHEST, preferred_element_type=F32)
 
 
 def decay_tile(d):
@@ -77,19 +78,19 @@
         for copy in halo_copies:
             copy.start()
     gate_copy.wait()
-    rows, cols = cumulative(gate_ref[...])
+    rows = cumulative(gate_ref[...])
+    heads, tails = jnp.exp(rows), jnp.exp(rows[:, DH - 1 :] - rows)
     for j in range(HALF):
-        if j % STEP == 0:
-            for copy in copies[j // STEP]:
-                copy.wait()
+        if j % GROUP == 0:
+            for step in copies[j // STEP : (j + GROUP) // STEP]:
+                for copy in step:
+                    copy.wait()
         at = slice(j * DH, (j + 1) * DH)
         last = rows[j : j + 1, DH - 1 : DH]
-        head = jnp.exp(cols[:, j : j + 1])
-        tail = jnp.exp(last - cols[:, j : j + 1])
-        kt = (k_ref[:, at].astype(F32) * tail).astype(BF16)
-        qh = (q_ref[:, at].astype(F32) * head).astype(BF16)
-        s = dot(kt, v_ref[:, at], 0, 0).astype(BF16)
-        g = dot(qh, g_ref[:, at], 0, 0).astype(BF16)
+        kt = (k_ref[:, at].T.astype(F32) * tails[j : j + 1]).astype(BF16)
+        qh = (q_ref[:, at].T.astype(F32) * heads[j : j + 1]).astype(BF16)
+        s = dot(kt, v_ref[:, at], 1, 0).astype(BF16)
+        g = dot(qh, g_ref[:, at], 1, 0).astype(BF16)
         d = decay_tile(jnp.exp(last))
         for r in range(2):
             part = slice(r * 64, (r + 1) * 64)
@@ -186,7 +187,7 @@
 
 def window_kernel(lin_scale, live_ref, q_hbm, k_hbm, v_hbm, g_hbm, halo_ref, gate_hbm, *rest):
     outs, row_ref = rest[:5], rest[5]
-    q_ref, k_ref, v_ref, g_ref, *stages, gate_ref, sems, out_sems, gate_sem = rest[6:]
+    q_ref, k_ref, v_ref, g_ref, *stages, a_ref, b_ref, w1_ref, w2_ref, lin_ref, win_ref, gate_ref, sems, out_sems, gate_sem = rest[6:]
     o_ref, qg_ref, kg_ref, vg_ref, back_ref = stages
     gate_copy = pltpu.make_async_copy(gate_hbm, gate_ref, gate_sem)
     gate_copy.start()
@@ -200,7 +201,7 @@
         ]
 
     def out_copies(i):
-        at = pl.ds(pl.multiple_of(i * width, width), width)
+        at = pl.ds(pl.multiple_of(i * 2 * DH, 2 * DH), 2 * DH)
         return [pltpu.make_async_copy(stage.at[:, at], out.at[:, at], out_sems.at[i, n]) for n, (stage, out) in enumerate(zip(stages, outs, strict=True))]
 
     for i in range(16 // WSTEP):
@@ -213,31 +214,42 @@
     causal = (key >= 0) & (key <= t)
     banded = (key > t - W) & (key <= t) & ((key >= 0) | live)
     scale = DH**-0.5
-    lin_bias = jnp.where(causal, math.log(lin_scale), -jnp.inf)
-    win_bias = jnp.where(banded, 0.0, -jnp.inf)
+    lin_ref[...] = jnp.where(causal, math.log(lin_scale), -jnp.inf)
+    win_ref[...] = jnp.where(banded, 0.0, -jnp.inf)
     gate_copy.wait()
-    row_ref[...] = cumulative(gate_ref[...])[0]
+    row_ref[...] = cumulative(gate_ref[...])
 
     def step(i, carry):
         for copy in copies(i):
             copy.wait()
-        for j in range(WSTEP):
-            at = pl.ds(pl.multiple_of(i * width + j * DH, DH), DH)
+        heads = [pl.ds(pl.multiple_of(i * width + j * DH, DH), DH) for j in range(WSTEP)]
+        for j, at in enumerate(heads):
             q, k, v, g = q_ref[:, at], k_ref[:, at], v_ref[:, at], g_ref[:, at]
             kx = jnp.concatenate([halo_ref[0:W, at], k[0:W]], axis=0)
             vx = jnp.concatenate([halo_ref[W : 2 * W, at], v[0:W]], axis=0)
-            a = jnp.concatenate([dot(q[0:W], kx, 1, 1), dot(q[W:], k, 1, 1)], axis=0)
-            b = jnp.concatenate([dot(g[0:W], vx, 1, 1), dot(g[W:], v, 1, 1)], axis=0)
-            row = jnp.broadcast_to(row_ref[pl.ds(i * WSTEP + j, 1), :], (DH, DH))
-            shifted = jnp.concatenate([row[:W, W:], row[:W, :W]], axis=1)
-            gap = row.T - jnp.concatenate([shifted, row[W:]], axis=0)
-            decay = jnp.exp(gap + lin_bias)
-            logits = a * scale + win_bias
+            a_ref[j, 0:W] = dot(q[0:W], kx, 1, 1)
+            a_ref[j, W:] = dot(q[W:], k, 1, 1)
+            b_ref[j, 0:W] = dot(g[0:W], vx, 1, 1)
+            b_ref[j, W:] = dot(g[W:], v, 1, 1)
+        rows = row_ref[pl.ds(i * WSTEP, WSTEP), :]
+        cols = rows.T
+        for j in range(WSTEP):
+            row = rows[j : j + 1, :]
+            shifted = jnp.concatenate([row[:, W:], row[:, :W]], axis=1)
+            keys = jnp.concatenate([jnp.broadcast_to(shifted, (W, DH)), jnp.broadcast_to(row, (W, DH))], axis=0)
+            a, b = a_ref[j], b_ref[j]
+            decay = jnp.exp(cols[:, j : j + 1] - keys + lin_ref[...])
+            logits = a * scale + win_ref[...]
             e = jnp.exp(logits - jnp.max(logits, axis=1, keepdims=True))
             inv = 1.0 / jnp.sum(e, axis=1, keepdims=True)
             delta = jnp.sum(e * b, axis=1, keepdims=True) * inv
-            w1 = (e * inv + decay * a).astype(BF16)
-            w2 = (e * (inv * scale) * (b - delta) + decay * b).astype(BF16)
+            w1_ref[j] = (e * inv + decay * a).astype(BF16)
+            w2_ref[j] = (e * (inv * scale) * (b - delta) + decay * b).astype(BF16)
+        for j, at in enumerate(heads):
+            q, k, v, g = q_ref[:, at], k_ref[:, at], v_ref[:, at], g_ref[:, at]
+            kx = jnp.concatenate([halo_ref[0:W, at], k[0:W]], axis=0)
+            vx = jnp.concatenate([halo_ref[W : 2 * W, at], v[0:W]], axis=0)
+            w1, w2 = w1_ref[j], w2_ref[j]
             o_ref[0:W, at] = dot(w1[0:W], vx, 1, 0)
             o_ref[W:, at] = dot(w1[W:], v, 1, 0)
             qg_ref[0:W, at] = dot(w2[0:W], kx, 1, 0)
@@ -252,31 +264,37 @@
             vg_ref[W:, at] = v_low[W:]
             back_ref[0:W, at] = k_top[0:W].astype(BF16)
             back_ref[W : 2 * W, at] = v_top[0:W].astype(BF16)
-        for copy in out_copies(i):
-            copy.start()
+            if j % 2 == 1:
+                for copy in out_copies(i * (WSTEP // 2) + j // 2):
+                    copy.start()
         return carry
 
     lax.fori_loop(0, 16 // WSTEP, step, 0)
-    for i in range(16 // WSTEP):
+    for i in range(8):
         for copy in out_copies(i):
             copy.wait()
 
 
-def final_kernel(lin_scale, n_alias, sel_ref, q_ref, k_ref, v_ref, g_ref, ret_hbm, row_ref, st_ref, po_ref, pq_ref, pk_ref, pv_ref, *rest):
+def final_kernel(lin_scale, n_alias, sel_ref, q_ref, k_hbm, v_hbm, g_ref, ret_hbm, row_ref, st_ref, po_ref, pq_ref, pk_hbm, pv_hbm, *rest):
     outs = rest[n_alias : n_alias + 4]
-    stage_ref, ret_ref, sems, ret_sem = rest[n_alias + 4 :]
+    stage_ref, k_ref, v_ref, ret_ref, pk_ref, pv_ref, sems, in_sems = rest[n_alias + 4 :]
     sel = sel_ref[0]
-    ret_copy = pltpu.make_async_copy(ret_hbm.at[:, pl.ds(pl.multiple_of(sel * COLS, COLS), COLS)], ret_ref, ret_sem)
-    ret_copy.start()
+    half = pl.ds(pl.multiple_of(sel * COLS, COLS), COLS)
+    late = [
+        pltpu.make_async_copy(big.at[:, half], small, in_sems.at[n])
+        for n, (big, small) in enumerate(((v_hbm, v_ref), (pk_hbm, pk_ref), (k_hbm, k_ref), (pv_hbm, pv_ref), (ret_hbm, ret_ref)))
+    ]
+    for copy in late:
+        copy.start()
     rows = row_ref[pl.ds(pl.multiple_of(sel * HALF, HALF), HALF), :]
     heads = jnp.exp(rows).T * lin_scale
     tails = jnp.exp(rows[:, DH - 1 :] - rows).T * lin_scale
-    width = STEP * DH
+    width = OSTEP * DH
     copies = []
 
     def send(n, j):
-        if j % STEP == STEP - 1:
-            i = j // STEP
+        if j % OSTEP == OSTEP - 1:
+            i = j // OSTEP
             target = pl.ds(pl.multiple_of(sel * COLS + i * width, width), width)
             copy = pltpu.make_async_copy(stage_ref.at[n, :, i * width : (i + 1) * width], outs[n].at[:, target], sems.at[i, n])
             copy.start()
@@ -291,14 +309,14 @@
         stage_ref[1, :, to] = (pq_ref[:, at] + head * dot(g_ref[:, at], s, 1, 1)).astype(BF16)
         send(0, j)
         send(1, j)
-    ret_copy.wait()
+    for copy in late:
+        copy.wait()
     for j in range(HALF):
-        at = pl.ds(pl.multiple_of(sel * COLS + j * DH, DH), DH)
         to = slice(j * DH, (j + 1) * DH)
         tail = tails[:, j : j + 1]
         m = jnp.concatenate([st_ref[2 * j, 64:128, :], st_ref[2 * j + 1, 64:128, :]], axis=0)
-        kg = pk_ref[:, at] + tail * dot(v_ref[:, at], m, 1, 1)
-        vg = pv_ref[:, at] + tail * dot(k_ref[:, at], m, 1, 0)
+        kg = pk_ref[:, to] + tail * dot(v_ref[:, to], m, 1, 1)
+        vg = pv_ref[:, to] + tail * dot(k_ref[:, to], m, 1, 0)
         stage_ref[2, 0:W, to] = kg[0:W].astype(BF16)
         stage_ref[2, W:, to] = (kg[W:] + ret_ref[0:W, to].astype(F32)).astype(BF16)
         stage_ref[3, 0:W, to] = vg[0:W].astype(BF16)
@@ -362,7 +380,10 @@
         out_specs=(IN_HBM,) * 5 + (IN_VMEM,),
         scratch_shapes=[pltpu.VMEM(full, BF16)] * 4
         + [pltpu.VMEM(full, F32)] * 4
-        + [pltpu.VMEM(full, BF16), pltpu.VMEM((16, DH), F32), DMA((steps, 4)), DMA((steps, 5)), DMA],
+        + [pltpu.VMEM(full, BF16)]
+        + [pltpu.VMEM((WSTEP, DH, DH), t) for t in (F32, F32, BF16, BF16)]
+        + [pltpu.VMEM((DH, DH), F32)] * 2
+        + [pltpu.VMEM((16, DH), F32), DMA((steps, 4)), DMA((8, 5)), DMA],
         cost_estimate=cost(6e8, 8e6),
         compiler_params=vmem(14),
         name="window",
@@ -374,9 +395,9 @@
     return pl.pallas_call(
         lambda *refs: final_kernel(lin_scale, n, *refs),
         out_shape=tuple(pltpu.HBM((128, 2048), BF16) for _ in range(4)),
-        in_specs=[IN_SMEM] + [IN_VMEM] * 4 + [IN_HBM] + [IN_VMEM] * 6 + [IN_HBM] * n,
+        in_specs=[IN_SMEM, IN_VMEM, IN_HBM, IN_HBM, IN_VMEM, IN_HBM] + [IN_VMEM] * 4 + [IN_HBM] * (2 + n),
         out_specs=(IN_HBM,) * 4,
-        scratch_shapes=[pltpu.VMEM((4, 128, COLS), BF16), pltpu.VMEM((128, COLS), BF16), DMA((HALF // STEP, 4)), DMA],
+        scratch_shapes=[pltpu.VMEM((4, 128, COLS), BF16)] + [pltpu.VMEM((128, COLS), BF16)] * 3 + [pltpu.VMEM((128, COLS), F32)] * 2 + [DMA((HALF // OSTEP, 4)), DMA((5,))],
         input_output_aliases={12 + i: i for i in range(n)},
         cost_estimate=cost(3e8, 5e6),
         compiler_params=vmem(8),
@@ -392,7 +413,7 @@
     z = lax.axis_index("z")[None].astype(jnp.int32)
     live = (lax.axis_index(AXES) > 0)[None].astype(jnp.int32)
     swap = [(0, 1), (1, 0)]
-    late = (q, k, v, g)
+    q_late, g_late = q, g
     q, k, v, g, gates = (pltpu.with_memory_space_constraint(a, pltpu.HBM) for a in (q, k, v, g, gates))
 
     sent, edge = local_states(theirs, q, k, v, g, gates, True)
@@ -409,8 +430,9 @@
     chip_in = lax.all_to_all(incoming, ("x", "y"), 0, 0, tiled=True)
     st_mine, st_theirs = small_call(hand_kernel, mine, (chip_in, own, other), [(PLANE, DH, DH)] * 2)
     st_other = lax.ppermute(st_theirs, "c", swap)
-    outs = finish(lin_scale, mine, *late, ret, sums, st_mine, parts, ())
-    return finish(lin_scale, theirs, *late, ret, sums, st_other, parts, outs)
+    parts[2:] = [pltpu.with_memory_space_constraint(a, pltpu.HBM) for a in parts[2:]]
+    outs = finish(lin_scale, mine, q_late, k, v, g_late, ret, sums, st_mine, parts, ())
+    return finish(lin_scale, theirs, q_late, k, v, g_late, ret, sums, st_other, parts, outs)
 
 
 def solution(mesh):

time: 86.1 us -> 77.2 us (0.90)
  Pallas kernels: 24.7 us -> 18.9 us
  local copies, waits for them, and re-layouts: 4.92 us -> 2.46 us
  waiting for transfers between devices: 22.2 us -> 20.5 us
  starting transfers between devices: 32.7 us -> 33.9 us
    pallas_call x1, Pallas kernels: 10.9 us -> 6.65 us  [window(): pl.pallas_call(lambda *refs: window_kernel(lin_scale, *refs), out_shape=t...]
    pallas_call x2, Pallas kernels: 7.14 us -> 3.47 us  [local_states(): pl.pallas_call(lambda *refs: states_kernel(with_halo, *refs), out_shape=t...]
    unnamed x16 -> x8, local copies, waits for them, and re-layouts: 4.92 us -> 2.46 us
    pallas_call x2, Pallas kernels: 3.56 us -> 5.64 us  [finish(): pl.pallas_call(lambda *refs: final_kernel(lin_scale, n, *refs), out_shape...]
    all_to_all x1, waiting for transfers between devices: 8.41 us -> 7.09 us  [per_device(): plane = lax.all_to_all(chip, ('x', 'y'), 0, 0, tiled=True)]
    ppermute x1, starting transfers between devices: 9.3 us -> 10.6 us  [per_device(): halo = lax.ppermute(edge, AXES, [(i, i + 1) for i in range(255)])]
  transfers between devices with their start and end apart: 7 -> 7, of which waited for: 2 -> 2; matrix products, arithmetic and copies ran while one was open for 0% -> 0% of each run, Pallas kernels for 20% -> 16%
where the time goes in v3:
time: 77.2 us; the launch traced here: 76.6 us
  starting transfers between devices  33.9 us (44%)
  waiting for transfers between devices  20.5 us (27%)
  Pallas kernels  18.9 us (24%)
  local copies, waits for them, and re-layouts  2.46 us (3%)
    ppermute x1, waiting for transfers between devices, per_device(): ret = lax.ppermute(back, AXES, [(i + 1, i) for i in range(255)])  13.4 us
    ppermute x1, starting transfers between devices, per_device(): halo = lax.ppermute(edge, AXES, [(i, i + 1) for i in range(255)])  10.6 us
    all_to_all x1, starting transfers between devices, per_device(): planes = lax.all_to_all(total, 'z', 0, 0, tiled=True)  7.1 us
    all_to_all x1, waiting for transfers between devices, per_device(): plane = lax.all_to_all(chip, ('x', 'y'), 0, 0, tiled=True)  7.09 us
    pallas_call x1, Pallas kernels, window(): pl.pallas_call(lambda *refs: window_kernel(lin_scale, *refs), out_shape=t...  6.65 us
    all_to_all x1, starting transfers between devices, per_device(): plane = lax.all_to_all(chip, ('x', 'y'), 0, 0, tiled=True)  6.53 us
    all_to_all x1, starting transfers between devices, per_device(): chip_in = lax.all_to_all(incoming, ('x', 'y'), 0, 0, tiled=True)  6.08 us
    pallas_call x2, Pallas kernels, finish(): pl.pallas_call(lambda *refs: final_kernel(lin_scale, n, *refs), out_shape...  5.64 us
  transfers between devices with their start and end apart: 7, of which 2 were waited for; matrix products, arithmetic and copies ran while one was open for 0% of the time, Pallas kernels for 16%

profile of v3, /device:TPU:127, one launch (start us, length us, event | category | flops | bytes accessed | tf_op | source)
XLA Modules:
  0.0 76.6 jit_solution(12797250835675971064)
XLA Ops:
  0.6 1.8 %local_states.2 = (bf16[16,144,128]{2,1,0:T(8,128)(2,1)S(1)}, bf16[128,2048]{1,0:T(8,128)(2,1)S(1)}) custom-call(s32[1]{0:T(128)S(6)} %sub.3.refs_0_, bf16[128,2048]{1,0:T(8,128)(2,1)} %refs_1_.9, bf16[128,2048]{1,0:T(8,128)(2,1)} %refs_2_.9, bf16[128,2048]{1,0:T(8,128)(2,1)} %refs_3_.9, bf16[128,2048]{1,0:T(8,128)(2,1)} %refs_4_.9, f32[16,128]{1,0:T(8,128)} %refs_5_.3), custom_call_target="tpu_custom_call" | custom-call | flops 70000000 | bytes 1600000 | tf_op jit(solution)/shard_map/local_states/pallas_call | solution.py:350
  2.5 0.7 collective-permute-start.2
  3.1 1.6 %local_states.3.own_ref = bf16[16,144,128]{2,1,0:T(8,128)(2,1)S(1)} custom-call(s32[1]{0:T(128)} %bitcast.refs_0_.c_ref, bf16[128,2048]{1,0:T(8,128)(2,1)} %refs_1_.9, bf16[128,2048]{1,0:T(8,128)(2,1)} %refs_2_.9, bf16[128,2048]{1,0:T(8,128)(2,1)} %refs_3_.9, bf16[128,2048]{1,0:T(8,128)(2,1)} %refs_4_.9, f32[16,128]{1,0:T(8,128)} %refs_5_.3), custom_call_target="tpu_custom_call" | custom-call | flops 70000000 | bytes 1600000 | tf_op jit(solution)/shard_map/local_states/pallas_call | solution.py:350
  4.8 0.0 collective-permute-done.2.other_ref
  4.8 1.1 %shard_map.84 = (bf16[16,144,128]{2,1,0:T(8,128)(2,1)}, bf16[16,144,128]{2,1,0:T(8,128)(2,1)S(1)}) custom-call(s32[1]{0:T(128)} %bitcast.refs_0_.c_ref, bf16[16,144,128]{2,1,0:T(8,128)(2,1)S(1)} %local_states.3.own_ref, bf16[16,144,128]{2,1,0:T(8,128)(2,1)S(1)} %collective-permute-done.2.other_ref), custom_call_target="tpu_custom_call" | custom-call | flops 1000000 | bytes 2000000 | tf_op jit(solution)/shard_map/pallas_call | solution.py:363
  5.9 6.5 %all-to-all-start = ((bf16[16,144,128]{2,1,0:T(8,128)(2,1)}), bf16[16,144,128]{2,1,0:T(8,128)(2,1)S(1)}, u32[]{:S(2)}, u32[]{:S(2)}) async-start(bf16[16,144,128]{2,1,0:T(8,128)(2,1)} %get-tuple-element.24), calls=%async_computation | async-start | bytes 1179648 | tf_op jit(solution)/shard_map/all_to_all | solution.py:424
  12.4 7.1 %all-to-all-done.msg_ref = bf16[16,144,128]{2,1,0:T(8,128)(2,1)S(1)} async-done(((bf16[16,144,128]{2,1,0:T(8,128)(2,1)}), bf16[16,144,128]{2,1,0:T(8,128)(2,1)S(1)}, u32[]{:S(2)}, u32[]{:S(2)}) %all-to-all-start) | async-done | bytes 589856 | tf_op jit(solution)/shard_map/all_to_all | solution.py:424
  19.5 0.8 %shard_map.85 = bf16[8,80,128]{2,1,0:T(8,128)(2,1)} custom-call(s32[1]{0:T(128)} %bitcast.2.z_ref, bf16[16,144,128]{2,1,0:T(8,128)(2,1)S(1)} %all-to-all-done.msg_ref), custom_call_target="tpu_custom_call" | custom-call | flops 1000000 | bytes 2000000 | tf_op jit(solution)/shard_map/pallas_call | solution.py:363
  20.3 7.1 %all-to-all-start.1 = ((bf16[8,80,128]{2,1,0:T(8,128)(2,1)}), bf16[8,80,128]{2,1,0:T(8,128)(2,1)S(1)}, u32[]{:S(2)}, u32[]{:S(2)}) async-start(bf16[8,80,128]{2,1,0:T(8,128)(2,1)} %shard_map.85), calls=%async_computation.1 | async-start | bytes 327680 | tf_op jit(solution)/shard_map/all_to_all | solution.py:427
  27.4 10.6 %collective-permute-start = (bf16[128,2048]{1,0:T(8,128)(2,1)S(1)}, bf16[128,2048]{1,0:T(8,128)(2,1)S(1)}, u32[]{:S(2)}, u32[]{:S(2)}) collective-permute-start(bf16[128,2048]{1,0:T(8,128)(2,1)S(1)} %get-tuple-element.20), channel_id=1, source_target_pairs={{0,1},{1,2},{2,3},{3,4},{4,5},{5,6},{6,7},{7,8},{8,9},{9,10},{10,1... | collective-permute-start | bytes 1572872 | tf_op jit(solution)/shard_map/ppermute | solution.py:421
  38.0 1.0 %shard_map.86 = bf16[16,128,128]{2,1,0:T(8,128)(2,1)} custom-call(s32[1]{0:T(128)} %bitcast.2.z_ref, bf16[16,144,128]{2,1,0:T(8,128)(2,1)S(1)} %all-to-all-done.msg_ref, bf16[8,80,128]{2,1,0:T(8,128)(2,1)S(1)} %all-to-all-done.1.planes_ref), custom_call_target="tpu_custom_call" | custom-call | flops 1000000 | bytes 2000000 | tf_op jit(solution)/shard_map/pallas_call | solution.py:363
  39.1 6.1 %all-to-all-start.2 = ((bf16[16,128,128]{2,1,0:T(8,128)(2,1)}), bf16[16,128,128]{2,1,0:T(8,128)(2,1)S(1)}, u32[]{:S(2)}, u32[]{:S(2)}) async-start(bf16[16,128,128]{2,1,0:T(8,128)(2,1)} %shard_map.86), calls=%async_computation.2 | async-start | bytes 1048576 | tf_op jit(solution)/shard_map/all_to_all | solution.py:430
  45.2 0.0 collective-permute-done.refs_5_
  45.2 6.7 %window.1 = (f32[128,2048]{1,0:T(8,128)}, f32[128,2048]{1,0:T(8,128)}, f32[128,2048]{1,0:T(8,128)}, f32[128,2048]{1,0:T(8,128)}, bf16[128,2048]{1,0:T(8,128)(2,1)}, /*index=5*/f32[16,128]{1,0:T(8,128)S(1)}) custom-call(s32[1]{0:T(128)} %bitcast.1.refs_0_, bf16[128,2048]{1,0:T(8,128)(2,1)} %refs_1_.9, bf16[128,2048]{1,0:T(8,128)(2,1)} %refs_2_.9, ...), custom_call_target="tpu_custom_call" | custom-call | flops 600000000 | bytes 8000000 | tf_op jit(solution)/shard_map/window/pallas_call | solution.py:376
  51.8 1.9 %collective-permute-start.1 = (bf16[128,2048]{1,0:T(8,128)(2,1)}, bf16[128,2048]{1,0:T(8,128)(2,1)S(1)}, u32[]{:S(2)}, u32[]{:S(2)}) collective-permute-start(bf16[128,2048]{1,0:T(8,128)(2,1)} %get-tuple-element.21), channel_id=1, source_target_pairs={{1,0},{2,1},{3,2},{4,3},{5,4},{6,5},{7,6},{8,7},{9,8},{10,9},{11,1... | collective-permute-start | bytes 1572872 | tf_op jit(solution)/shard_map/ppermute | solution.py:428
  53.8 0.0 copy-start
  53.8 0.0 copy-start.1
  53.8 0.2 shard_map.87
  54.0 1.1 %collective-permute-start.3 = (bf16[16,128,128]{2,1,0:T(8,128)(2,1)S(1)}, bf16[16,128,128]{2,1,0:T(8,128)(2,1)S(1)}, u32[]{:S(2)}, u32[]{:S(2)}) collective-permute-start(bf16[16,128,128]{2,1,0:T(8,128)(2,1)S(1)} %get-tuple-element.26), channel_id=1, source_target_pairs={{0,1},{1,0},{2,3},{3,2},{4,5},{5,4},{6,7},{7,6},{8,9},{9,8},{10,11... | collective-permute-start | bytes 1572872 | tf_op jit(solution)/shard_map/ppermute | solution.py:432
  55.1 13.4 %collective-permute-done.1.refs_5_ = bf16[128,2048]{1,0:T(8,128)(2,1)S(1)} collective-permute-done((bf16[128,2048]{1,0:T(8,128)(2,1)}, bf16[128,2048]{1,0:T(8,128)(2,1)S(1)}, u32[]{:S(2)}, u32[]{:S(2)}) %collective-permute-start.1) | collective-permute-done | bytes 524320 | tf_op jit(solution)/shard_map/ppermute | solution.py:428
  68.5 1.2 %copy-done.2 = f32[128,2048]{1,0:T(8,128)S(1)} copy-done((f32[128,2048]{1,0:T(8,128)S(1)}, f32[128,2048]{1,0:T(8,128)}, u32[]{:S(2)}) %copy-start.2) | copy-done | bytes 1048600
  69.7 1.2 %copy-done.3 = f32[128,2048]{1,0:T(8,128)S(1)} copy-done((f32[128,2048]{1,0:T(8,128)S(1)}, f32[128,2048]{1,0:T(8,128)}, u32[]{:S(2)}) %copy-start.3) | copy-done | bytes 1048600
  70.9 2.8 %finish.2 = (bf16[128,2048]{1,0:T(8,128)(2,1)}, bf16[128,2048]{1,0:T(8,128)(2,1)}, bf16[128,2048]{1,0:T(8,128)(2,1)}, bf16[128,2048]{1,0:T(8,128)(2,1)}) custom-call(s32[1]{0:T(128)} %bitcast.refs_0_.c_ref, bf16[128,2048]{1,0:T(8,128)(2,1)S(1)} %copy-done, bf16[128,2048]{1,0:T(8,128)(2,1)} %refs_2_.9, bf16[128,2048]{1,0:T(8,128)(2,1)} %refs_3_.9, ...), custom_call_target="tpu_custom_call" | custom-call | flops 300000000 | bytes 5000000 | tf_op jit(solution)/shard_map/finish/pallas_call | solution.py:395
  73.8 2.8 %finish.3 = (bf16[128,2048]{1,0:T(8,128)(2,1)}, bf16[128,2048]{1,0:T(8,128)(2,1)}, bf16[128,2048]{1,0:T(8,128)(2,1)}, bf16[128,2048]{1,0:T(8,128)(2,1)}) custom-call(s32[1]{0:T(128)S(6)} %sub.3.refs_0_, bf16[128,2048]{1,0:T(8,128)(2,1)S(1)} %copy-done, ...), custom_call_target="tpu_custom_call", output_to_operand_aliasing={{0}: (12, {}), {1}: (13, {}), {2}: (14, {}), {3}: (15, {})} | custom-call | flops 300000000 | bytes 5000000 | tf_op jit(solution)/shard_map/finish/pallas_call | solution.py:395
  (7 shorter events, 0.0 us)
Async XLA Ops:
  2.5 2.3 %collective-permute-start.2 = (bf16[16,144,128]{2,1,0:T(8,128)(2,1)S(1)}, bf16[16,144,128]{2,1,0:T(8,128)(2,1)S(1)}, u32[]{:S(2)}, u32[]{:S(2)}) collective-permute-start(bf16[16,144,128]{2,1,0:T(8,128)(2,1)S(1)} %get-tuple-element.23), channel_id=1, source_target_pairs={{0,1},{1,0},{2,3},{3,2},{4,5},{5,4},{6,7},{7,6},{8,9},{9,8},{10,11... | collective-permute-start | bytes 1769480 | tf_op jit(solution)/shard_map/ppermute | solution.py:420
  5.9 13.6 %all-to-all-start = ((bf16[16,144,128]{2,1,0:T(8,128)(2,1)}), bf16[16,144,128]{2,1,0:T(8,128)(2,1)S(1)}, u32[]{:S(2)}, u32[]{:S(2)}) async-start(bf16[16,144,128]{2,1,0:T(8,128)(2,1)} %get-tuple-element.24), calls=%async_computation | async-start | bytes 1179648 | tf_op jit(solution)/shard_map/all_to_all | solution.py:424
  20.3 17.7 %all-to-all-start.1 = ((bf16[8,80,128]{2,1,0:T(8,128)(2,1)}), bf16[8,80,128]{2,1,0:T(8,128)(2,1)S(1)}, u32[]{:S(2)}, u32[]{:S(2)}) async-start(bf16[8,80,128]{2,1,0:T(8,128)(2,1)} %shard_map.85), calls=%async_computation.1 | async-start | bytes 327680 | tf_op jit(solution)/shard_map/all_to_all | solution.py:427
  27.4 17.7 %collective-permute-start = (bf16[128,2048]{1,0:T(8,128)(2,1)S(1)}, bf16[128,2048]{1,0:T(8,128)(2,1)S(1)}, u32[]{:S(2)}, u32[]{:S(2)}) collective-permute-start(bf16[128,2048]{1,0:T(8,128)(2,1)S(1)} %get-tuple-element.20), channel_id=1, source_target_pairs={{0,1},{1,2},{2,3},{3,4},{4,5},{5,6},{6,7},{7,8},{8,9},{9,10},{10,1... | collective-permute-start | bytes 1572872 | tf_op jit(solution)/shard_map/ppermute | solution.py:421
  39.1 14.7 %all-to-all-start.2 = ((bf16[16,128,128]{2,1,0:T(8,128)(2,1)}), bf16[16,128,128]{2,1,0:T(8,128)(2,1)S(1)}, u32[]{:S(2)}, u32[]{:S(2)}) async-start(bf16[16,128,128]{2,1,0:T(8,128)(2,1)} %shard_map.86), calls=%async_computation.2 | async-start | bytes 1048576 | tf_op jit(solution)/shard_map/all_to_all | solution.py:430
  51.8 16.7 %collective-permute-start.1 = (bf16[128,2048]{1,0:T(8,128)(2,1)}, bf16[128,2048]{1,0:T(8,128)(2,1)S(1)}, u32[]{:S(2)}, u32[]{:S(2)}) collective-permute-start(bf16[128,2048]{1,0:T(8,128)(2,1)} %get-tuple-element.21), channel_id=1, source_target_pairs={{1,0},{2,1},{3,2},{4,3},{5,4},{6,5},{7,6},{8,7},{9,8},{10,9},{11,1... | collective-permute-start | bytes 1572872 | tf_op jit(solution)/shard_map/ppermute | solution.py:428
  53.8 14.7 %copy-start = (bf16[128,2048]{1,0:T(8,128)(2,1)S(1)}, bf16[128,2048]{1,0:T(8,128)(2,1)}, u32[]{:S(2)}) copy-start(bf16[128,2048]{1,0:T(8,128)(2,1)} %refs_1_.9) | copy-start | bytes 1572868
  53.8 14.7 %copy-start.1 = (bf16[128,2048]{1,0:T(8,128)(2,1)S(1)}, bf16[128,2048]{1,0:T(8,128)(2,1)}, u32[]{:S(2)}) copy-start(bf16[128,2048]{1,0:T(8,128)(2,1)} %refs_4_.9) | copy-start | bytes 1572868
  54.0 19.7 %collective-permute-start.3 = (bf16[16,128,128]{2,1,0:T(8,128)(2,1)S(1)}, bf16[16,128,128]{2,1,0:T(8,128)(2,1)S(1)}, u32[]{:S(2)}, u32[]{:S(2)}) collective-permute-start(bf16[16,128,128]{2,1,0:T(8,128)(2,1)S(1)} %get-tuple-element.26), channel_id=1, source_target_pairs={{0,1},{1,0},{2,3},{3,2},{4,5},{5,4},{6,7},{7,6},{8,9},{9,8},{10,11... | collective-permute-start | bytes 1572872 | tf_op jit(solution)/shard_map/ppermute | solution.py:432
  68.5 1.2 %copy-start.2 = (f32[128,2048]{1,0:T(8,128)S(1)}, f32[128,2048]{1,0:T(8,128)}, u32[]{:S(2)}) copy-start(f32[128,2048]{1,0:T(8,128)} %get-tuple-element.27.refs_8_) | copy-start | bytes 3145732
  69.7 1.2 %copy-start.3 = (f32[128,2048]{1,0:T(8,128)S(1)}, f32[128,2048]{1,0:T(8,128)}, u32[]{:S(2)}) copy-start(f32[128,2048]{1,0:T(8,128)} %get-tuple-element.28.refs_9_) | copy-start | bytes 3145732

commit v4 on v3

--- a/solution.py
+++ b/solution.py
@@ -186,9 +186,11 @@
 
 
 def window_kernel(lin_scale, live_ref, q_hbm, k_hbm, v_hbm, g_hbm, halo_ref, gate_hbm, *rest):
-    outs, row_ref = rest[:5], rest[5]
-    q_ref, k_ref, v_ref, g_ref, *stages, a_ref, b_ref, w1_ref, w2_ref, lin_ref, win_ref, gate_ref, sems, out_sems, gate_sem = rest[6:]
-    o_ref, qg_ref, kg_ref, vg_ref, back_ref = stages
+    parts_hbm, inputs_hbm, back_hbm, row_ref = rest[:4]
+    inputs_ref, parts_ref, back_ref, a_ref, b_ref, w1_ref, w2_ref, lin_ref, win_ref, gate_ref, sems, out_sems, gate_sem, kept_sem = rest[4:]
+    q_ref, k_ref, v_ref, g_ref = (inputs_ref.at[n] for n in range(4))
+    o_ref, qg_ref, kg_ref, vg_ref = (parts_ref.at[n] for n in range(4))
+    kept = pltpu.make_async_copy(inputs_ref, inputs_hbm, kept_sem)
     gate_copy = pltpu.make_async_copy(gate_hbm, gate_ref, gate_sem)
     gate_copy.start()
     width = WSTEP * DH
@@ -202,7 +204,10 @@
 
     def out_copies(i):
         at = pl.ds(pl.multiple_of(i * 2 * DH, 2 * DH), 2 * DH)
-        return [pltpu.make_async_copy(stage.at[:, at], out.at[:, at], out_sems.at[i, n]) for n, (stage, out) in enumerate(zip(stages, outs, strict=True))]
+        return [
+            pltpu.make_async_copy(parts_ref.at[:, :, at], parts_hbm.at[:, :, at], out_sems.at[i, 0]),
+            pltpu.make_async_copy(back_ref.at[:, at], back_hbm.at[:, at], out_sems.at[i, 1]),
+        ]
 
     for i in range(16 // WSTEP):
         for copy in copies(i):
@@ -222,6 +227,8 @@
     def step(i, carry):
         for copy in copies(i):
             copy.wait()
+        if WSTEP == 16:
+            kept.start()
         heads = [pl.ds(pl.multiple_of(i * width + j * DH, DH), DH) for j in range(WSTEP)]
         for j, at in enumerate(heads):
             q, k, v, g = q_ref[:, at], k_ref[:, at], v_ref[:, at], g_ref[:, at]
@@ -250,18 +257,18 @@
             kx = jnp.concatenate([halo_ref[0:W, at], k[0:W]], axis=0)
             vx = jnp.concatenate([halo_ref[W : 2 * W, at], v[0:W]], axis=0)
             w1, w2 = w1_ref[j], w2_ref[j]
-            o_ref[0:W, at] = dot(w1[0:W], vx, 1, 0)
-            o_ref[W:, at] = dot(w1[W:], v, 1, 0)
-            qg_ref[0:W, at] = dot(w2[0:W], kx, 1, 0)
-            qg_ref[W:, at] = dot(w2[W:], k, 1, 0)
+            o_ref[0:W, at] = (dot(w1[0:W], vx, 1, 0)).astype(BF16)
+            o_ref[W:, at] = (dot(w1[W:], v, 1, 0)).astype(BF16)
+            qg_ref[0:W, at] = (dot(w2[0:W], kx, 1, 0)).astype(BF16)
+            qg_ref[W:, at] = (dot(w2[W:], k, 1, 0)).astype(BF16)
             k_top = dot(w2[0:W], q[0:W], 0, 0)
             k_low = dot(w2[W:], q[W:], 0, 0)
             v_top = dot(w1[0:W], g[0:W], 0, 0)
             v_low = dot(w1[W:], g[W:], 0, 0)
-            kg_ref[0:W, at] = k_low[0:W] + k_top[W:]
-            kg_ref[W:, at] = k_low[W:]
-            vg_ref[0:W, at] = v_low[0:W] + v_top[W:]
-            vg_ref[W:, at] = v_low[W:]
+            kg_ref[0:W, at] = (k_low[0:W] + k_top[W:]).astype(BF16)
+            kg_ref[W:, at] = (k_low[W:]).astype(BF16)
+            vg_ref[0:W, at] = (v_low[0:W] + v_top[W:]).astype(BF16)
+            vg_ref[W:, at] = (v_low[W:]).astype(BF16)
             back_ref[0:W, at] = k_top[0:W].astype(BF16)
             back_ref[W : 2 * W, at] = v_top[0:W].astype(BF16)
             if j % 2 == 1:
@@ -270,22 +277,20 @@
         return carry
 
     lax.fori_loop(0, 16 // WSTEP, step, 0)
+    if WSTEP < 16:
+        kept.start()
     for i in range(8):
         for copy in out_copies(i):
             copy.wait()
-
-
-def final_kernel(lin_scale, n_alias, sel_ref, q_ref, k_hbm, v_hbm, g_ref, ret_hbm, row_ref, st_ref, po_ref, pq_ref, pk_hbm, pv_hbm, *rest):
+    kept.wait()
+
+
+def final_kernel(lin_scale, n_alias, sel_ref, inputs_ref, ret_ref, row_ref, st_ref, parts_ref, *rest):
     outs = rest[n_alias : n_alias + 4]
-    stage_ref, k_ref, v_ref, ret_ref, pk_ref, pv_ref, sems, in_sems = rest[n_alias + 4 :]
+    stage_ref, sems = rest[n_alias + 4 :]
+    q_ref, k_ref, v_ref, g_ref = (inputs_ref.at[n] for n in range(4))
+    po_ref, pq_ref, pk_ref, pv_ref = (parts_ref.at[n] for n in range(4))
     sel = sel_ref[0]
-    half = pl.ds(pl.multiple_of(sel * COLS, COLS), COLS)
-    late = [
-        pltpu.make_async_copy(big.at[:, half], small, in_sems.at[n])
-        for n, (big, small) in enumerate(((v_hbm, v_ref), (pk_hbm, pk_ref), (k_hbm, k_ref), (pv_hbm, pv_ref), (ret_hbm, ret_ref)))
-    ]
-    for copy in late:
-        copy.start()
     rows = row_ref[pl.ds(pl.multiple_of(sel * HALF, HALF), HALF), :]
     heads = jnp.exp(rows).T * lin_scale
     tails = jnp.exp(rows[:, DH - 1 :] - rows).T * lin_scale
@@ -305,22 +310,21 @@
         to = slice(j * DH, (j + 1) * DH)
         head = heads[:, j : j + 1]
         s = jnp.concatenate([st_ref[2 * j, 0:64, :], st_ref[2 * j + 1, 0:64, :]], axis=0)
-        stage_ref[0, :, to] = (po_ref[:, at] + head * dot(q_ref[:, at], s, 1, 0)).astype(BF16)
-        stage_ref[1, :, to] = (pq_ref[:, at] + head * dot(g_ref[:, at], s, 1, 1)).astype(BF16)
+        stage_ref[0, :, to] = (po_ref[:, at].astype(F32) + head * dot(q_ref[:, at], s, 1, 0)).astype(BF16)
+        stage_ref[1, :, to] = (pq_ref[:, at].astype(F32) + head * dot(g_ref[:, at], s, 1, 1)).astype(BF16)
         send(0, j)
         send(1, j)
-    for copy in late:
-        copy.wait()
     for j in range(HALF):
+        at = pl.ds(pl.multiple_of(sel * COLS + j * DH, DH), DH)
         to = slice(j * DH, (j + 1) * DH)
         tail = tails[:, j : j + 1]
         m = jnp.concatenate([st_ref[2 * j, 64:128, :], st_ref[2 * j + 1, 64:128, :]], axis=0)
-        kg = pk_ref[:, to] + tail * dot(v_ref[:, to], m, 1, 1)
-        vg = pv_ref[:, to] + tail * dot(k_ref[:, to], m, 1, 0)
+        kg = pk_ref[:, at].astype(F32) + tail * dot(v_ref[:, at], m, 1, 1)
+        vg = pv_ref[:, at].astype(F32) + tail * dot(k_ref[:, at], m, 1, 0)
         stage_ref[2, 0:W, to] = kg[0:W].astype(BF16)
-        stage_ref[2, W:, to] = (kg[W:] + ret_ref[0:W, to].astype(F32)).astype(BF16)
+        stage_ref[2, W:, to] = (kg[W:] + ret_ref[0:W, at].astype(F32)).astype(BF16)
         stage_ref[3, 0:W, to] = vg[0:W].astype(BF16)
-        stage_ref[3, W:, to] = (vg[W:] + ret_ref[W : 2 * W, to].astype(F32)).astype(BF16)
+        stage_ref[3, W:, to] = (vg[W:] + ret_ref[W : 2 * W, at].astype(F32)).astype(BF16)
         send(2, j)
         send(3, j)
     for copy in copies:
@@ -375,34 +379,32 @@
     steps = 16 // WSTEP
     return pl.pallas_call(
         lambda *refs: window_kernel(lin_scale, *refs),
-        out_shape=tuple(pltpu.HBM(full, F32) for _ in range(4)) + (pltpu.HBM(full, BF16), pltpu.VMEM((16, DH), F32)),
+        out_shape=(pltpu.HBM((4, *full), BF16), pltpu.HBM((4, *full), BF16), pltpu.HBM(full, BF16), pltpu.VMEM((16, DH), F32)),
         in_specs=[IN_SMEM] + [IN_HBM] * 4 + [IN_VMEM, IN_HBM],
-        out_specs=(IN_HBM,) * 5 + (IN_VMEM,),
-        scratch_shapes=[pltpu.VMEM(full, BF16)] * 4
-        + [pltpu.VMEM(full, F32)] * 4
-        + [pltpu.VMEM(full, BF16)]
+        out_specs=(IN_HBM,) * 3 + (IN_VMEM,),
+        scratch_shapes=[pltpu.VMEM((4, *full), BF16), pltpu.VMEM((4, *full), BF16), pltpu.VMEM(full, BF16)]
         + [pltpu.VMEM((WSTEP, DH, DH), t) for t in (F32, F32, BF16, BF16)]
         + [pltpu.VMEM((DH, DH), F32)] * 2
-        + [pltpu.VMEM((16, DH), F32), DMA((steps, 4)), DMA((8, 5)), DMA],
+        + [pltpu.VMEM((16, DH), F32), DMA((steps, 4)), DMA((8, 2)), DMA, DMA],
         cost_estimate=cost(6e8, 8e6),
         compiler_params=vmem(14),
         name="window",
     )(live, q, k, v, g, halo, gates)
 
 
-def finish(lin_scale, sel, q, k, v, g, ret, rows, states, parts, previous):
+def finish(lin_scale, sel, inputs, ret, rows, states, parts, previous):
     n = len(previous)
     return pl.pallas_call(
         lambda *refs: final_kernel(lin_scale, n, *refs),
         out_shape=tuple(pltpu.HBM((128, 2048), BF16) for _ in range(4)),
-        in_specs=[IN_SMEM, IN_VMEM, IN_HBM, IN_HBM, IN_VMEM, IN_HBM] + [IN_VMEM] * 4 + [IN_HBM] * (2 + n),
+        in_specs=[IN_SMEM] + [IN_VMEM] * 5 + [IN_HBM] * n,
         out_specs=(IN_HBM,) * 4,
-        scratch_shapes=[pltpu.VMEM((4, 128, COLS), BF16)] + [pltpu.VMEM((128, COLS), BF16)] * 3 + [pltpu.VMEM((128, COLS), F32)] * 2 + [DMA((HALF // OSTEP, 4)), DMA((5,))],
-        input_output_aliases={12 + i: i for i in range(n)},
+        scratch_shapes=[pltpu.VMEM((4, 128, COLS), BF16), DMA((HALF // OSTEP, 4))],
+        input_output_aliases={6 + i: i for i in range(n)},
         cost_estimate=cost(3e8, 5e6),
         compiler_params=vmem(8),
         name="finish",
-    )(sel, q, k, v, g, ret, rows, states, *parts, *previous)
+    )(sel, inputs, ret, rows, states, parts, *previous)
 
 
 def per_device(q, k, v, g, gates):
@@ -413,7 +415,6 @@
     z = lax.axis_index("z")[None].astype(jnp.int32)
     live = (lax.axis_index(AXES) > 0)[None].astype(jnp.int32)
     swap = [(0, 1), (1, 0)]
-    q_late, g_late = q, g
     q, k, v, g, gates = (pltpu.with_memory_space_constraint(a, pltpu.HBM) for a in (q, k, v, g, gates))
 
     sent, edge = local_states(theirs, q, k, v, g, gates, True)
@@ -422,7 +423,7 @@
     (own,) = local_states(mine, q, k, v, g, gates, False)
     chip, other = small_call(combine_kernel, mine, (own, other), [(PLANE, MSG, DH)] * 2)
     plane = lax.all_to_all(chip, ("x", "y"), 0, 0, tiled=True)
-    *parts, back, sums = window(lin_scale, live, q, k, v, g, halo, gates)
+    parts, inputs, back, sums = window(lin_scale, live, q, k, v, g, halo, gates)
     (total,) = small_call(plane_kernel, z, (plane,), [(GRID[0], 80, DH)])
     planes = lax.all_to_all(total, "z", 0, 0, tiled=True)
     ret = lax.ppermute(back, AXES, [(i + 1, i) for i in range(255)])
@@ -430,9 +431,8 @@
     chip_in = lax.all_to_all(incoming, ("x", "y"), 0, 0, tiled=True)
     st_mine, st_theirs = small_call(hand_kernel, mine, (chip_in, own, other), [(PLANE, DH, DH)] * 2)
     st_other = lax.ppermute(st_theirs, "c", swap)
-    parts[2:] = [pltpu.with_memory_space_constraint(a, pltpu.HBM) for a in parts[2:]]
-    outs = finish(lin_scale, mine, q_late, k, v, g_late, ret, sums, st_mine, parts, ())
-    return finish(lin_scale, theirs, q_late, k, v, g_late, ret, sums, st_other, parts, outs)
+    outs = finish(lin_scale, mine, inputs, ret, sums, st_mine, parts, ())
+    return finish(lin_scale, theirs, inputs, ret, sums, st_other, parts, outs)
 
 
 def solution(mesh):

time: 77.2 us -> 75.9 us (0.983)
  Pallas kernels: 18.9 us -> 17 us
    pallas_call x2, Pallas kernels: 5.64 us -> 3.78 us  [finish(): pl.pallas_call(lambda *refs: final_kernel(lin_scale, n, *refs), out_shape...]
    unnamed x8 -> x6, local copies, waits for them, and re-layouts: 2.46 us -> 3.19 us
  transfers between devices with their start and end apart: 7 -> 7, of which waited for: 2 -> 2; matrix products, arithmetic and copies ran while one was open for 0% -> 0% of each run, Pallas kernels for 16% -> 15%
where the time goes in v4:
time: 75.9 us; the launch traced here: 75.4 us
  starting transfers between devices  33.9 us (45%)
  waiting for transfers between devices  20.5 us (27%)
  Pallas kernels  17 us (22%)
  local copies, waits for them, and re-layouts  3.19 us (4%)
    ppermute x1, waiting for transfers between devices, per_device(): ret = lax.ppermute(back, AXES, [(i + 1, i) for i in range(255)])  13.4 us
    ppermute x1, starting transfers between devices, per_device(): halo = lax.ppermute(edge, AXES, [(i, i + 1) for i in range(255)])  10.6 us
    all_to_all x1, starting transfers between devices, per_device(): planes = lax.all_to_all(total, 'z', 0, 0, tiled=True)  7.1 us
    all_to_all x1, waiting for transfers between devices, per_device(): plane = lax.all_to_all(chip, ('x', 'y'), 0, 0, tiled=True)  7.09 us
    pallas_call x1, Pallas kernels, window(): pl.pallas_call(lambda *refs: window_kernel(lin_scale, *refs), out_shape=(...  6.54 us
    all_to_all x1, starting transfers between devices, per_device(): plane = lax.all_to_all(chip, ('x', 'y'), 0, 0, tiled=True)  6.53 us
    all_to_all x1, starting transfers between devices, per_device(): chip_in = lax.all_to_all(incoming, ('x', 'y'), 0, 0, tiled=True)  6.08 us
    pallas_call x2, Pallas kernels, finish(): pl.pallas_call(lambda *refs: final_kernel(lin_scale, n, *refs), out_shape...  3.78 us
  transfers between devices with their start and end apart: 7, of which 2 were waited for; matrix products, arithmetic and copies ran while one was open for 0% of the time, Pallas kernels for 15%

profile of v4, /device:TPU:127, one launch (start us, length us, event | category | flops | bytes accessed | tf_op | source)
XLA Modules:
  0.0 75.4 jit_solution(4461404885431375227)
XLA Ops:
  0.6 1.8 %local_states.2 = (bf16[16,144,128]{2,1,0:T(8,128)(2,1)S(1)}, bf16[128,2048]{1,0:T(8,128)(2,1)S(1)}) custom-call(s32[1]{0:T(128)S(6)} %sub.3.refs_0_, bf16[128,2048]{1,0:T(8,128)(2,1)} %refs_1_.5, bf16[128,2048]{1,0:T(8,128)(2,1)} %refs_2_.5, bf16[128,2048]{1,0:T(8,128)(2,1)} %refs_3_.5, bf16[128,2048]{1,0:T(8,128)(2,1)} %refs_4_.5, f32[16,128]{1,0:T(8,128)} %refs_5_.3), custom_call_target="tpu_custom_call" | custom-call | flops 70000000 | bytes 1600000 | tf_op jit(solution)/shard_map/local_states/pallas_call | solution.py:354
  2.5 0.7 collective-permute-start.2
  3.1 1.6 %local_states.3.own_ref = bf16[16,144,128]{2,1,0:T(8,128)(2,1)S(1)} custom-call(s32[1]{0:T(128)} %bitcast.refs_0_.c_ref, bf16[128,2048]{1,0:T(8,128)(2,1)} %refs_1_.5, bf16[128,2048]{1,0:T(8,128)(2,1)} %refs_2_.5, bf16[128,2048]{1,0:T(8,128)(2,1)} %refs_3_.5, bf16[128,2048]{1,0:T(8,128)(2,1)} %refs_4_.5, f32[16,128]{1,0:T(8,128)} %refs_5_.3), custom_call_target="tpu_custom_call" | custom-call | flops 70000000 | bytes 1600000 | tf_op jit(solution)/shard_map/local_states/pallas_call | solution.py:354
  4.8 0.0 collective-permute-done.2.other_ref
  4.8 1.1 %shard_map.84 = (bf16[16,144,128]{2,1,0:T(8,128)(2,1)}, bf16[16,144,128]{2,1,0:T(8,128)(2,1)S(1)}) custom-call(s32[1]{0:T(128)} %bitcast.refs_0_.c_ref, bf16[16,144,128]{2,1,0:T(8,128)(2,1)S(1)} %local_states.3.own_ref, bf16[16,144,128]{2,1,0:T(8,128)(2,1)S(1)} %collective-permute-done.2.other_ref), custom_call_target="tpu_custom_call" | custom-call | flops 1000000 | bytes 2000000 | tf_op jit(solution)/shard_map/pallas_call | solution.py:367
  5.9 6.5 %all-to-all-start = ((bf16[16,144,128]{2,1,0:T(8,128)(2,1)}), bf16[16,144,128]{2,1,0:T(8,128)(2,1)S(1)}, u32[]{:S(2)}, u32[]{:S(2)}) async-start(bf16[16,144,128]{2,1,0:T(8,128)(2,1)} %get-tuple-element.23), calls=%async_computation | async-start | bytes 1179648 | tf_op jit(solution)/shard_map/all_to_all | solution.py:425
  12.4 7.1 %all-to-all-done.msg_ref = bf16[16,144,128]{2,1,0:T(8,128)(2,1)S(1)} async-done(((bf16[16,144,128]{2,1,0:T(8,128)(2,1)}), bf16[16,144,128]{2,1,0:T(8,128)(2,1)S(1)}, u32[]{:S(2)}, u32[]{:S(2)}) %all-to-all-start) | async-done | bytes 589856 | tf_op jit(solution)/shard_map/all_to_all | solution.py:425
  19.5 0.8 %shard_map.85 = bf16[8,80,128]{2,1,0:T(8,128)(2,1)} custom-call(s32[1]{0:T(128)} %bitcast.2.z_ref, bf16[16,144,128]{2,1,0:T(8,128)(2,1)S(1)} %all-to-all-done.msg_ref), custom_call_target="tpu_custom_call" | custom-call | flops 1000000 | bytes 2000000 | tf_op jit(solution)/shard_map/pallas_call | solution.py:367
  20.3 7.1 %all-to-all-start.1 = ((bf16[8,80,128]{2,1,0:T(8,128)(2,1)}), bf16[8,80,128]{2,1,0:T(8,128)(2,1)S(1)}, u32[]{:S(2)}, u32[]{:S(2)}) async-start(bf16[8,80,128]{2,1,0:T(8,128)(2,1)} %shard_map.85), calls=%async_computation.1 | async-start | bytes 327680 | tf_op jit(solution)/shard_map/all_to_all | solution.py:428
  27.4 10.6 %collective-permute-start = (bf16[128,2048]{1,0:T(8,128)(2,1)S(1)}, bf16[128,2048]{1,0:T(8,128)(2,1)S(1)}, u32[]{:S(2)}, u32[]{:S(2)}) collective-permute-start(bf16[128,2048]{1,0:T(8,128)(2,1)S(1)} %get-tuple-element.18), channel_id=1, source_target_pairs={{0,1},{1,2},{2,3},{3,4},{4,5},{5,6},{6,7},{7,8},{8,9},{9,10},{10,1... | collective-permute-start | bytes 1572872 | tf_op jit(solution)/shard_map/ppermute | solution.py:422
  38.0 0.0 all-to-all-done.1.planes_ref
  38.0 1.0 %shard_map.86 = bf16[16,128,128]{2,1,0:T(8,128)(2,1)} custom-call(s32[1]{0:T(128)} %bitcast.2.z_ref, bf16[16,144,128]{2,1,0:T(8,128)(2,1)S(1)} %all-to-all-done.msg_ref, bf16[8,80,128]{2,1,0:T(8,128)(2,1)S(1)} %all-to-all-done.1.planes_ref), custom_call_target="tpu_custom_call" | custom-call | flops 1000000 | bytes 2000000 | tf_op jit(solution)/shard_map/pallas_call | solution.py:367
  39.1 6.1 %all-to-all-start.2 = ((bf16[16,128,128]{2,1,0:T(8,128)(2,1)}), bf16[16,128,128]{2,1,0:T(8,128)(2,1)S(1)}, u32[]{:S(2)}, u32[]{:S(2)}) async-start(bf16[16,128,128]{2,1,0:T(8,128)(2,1)} %shard_map.86), calls=%async_computation.2 | async-start | bytes 1048576 | tf_op jit(solution)/shard_map/all_to_all | solution.py:431
  45.2 0.0 collective-permute-done.refs_5_
  45.2 6.5 %window.1 = (bf16[4,128,2048]{2,1,0:T(8,128)(2,1)}, bf16[4,128,2048]{2,1,0:T(8,128)(2,1)}, bf16[128,2048]{1,0:T(8,128)(2,1)}, f32[16,128]{1,0:T(8,128)S(1)}) custom-call(s32[1]{0:T(128)} %bitcast.1.refs_0_, bf16[128,2048]{1,0:T(8,128)(2,1)} %refs_1_.5, bf16[128,2048]{1,0:T(8,128)(2,1)} %refs_2_.5, bf16[128,2048]{1,0:T(8,128)(2,1)} %refs_3_.5, ...), custom_call_target="tpu_custom_call" | custom-call | flops 600000000 | bytes 8000000 | tf_op jit(solution)/shard_map/window/pallas_call | solution.py:380
  51.7 1.9 %collective-permute-start.1 = (bf16[128,2048]{1,0:T(8,128)(2,1)}, bf16[128,2048]{1,0:T(8,128)(2,1)S(1)}, u32[]{:S(2)}, u32[]{:S(2)}) collective-permute-start(bf16[128,2048]{1,0:T(8,128)(2,1)} %get-tuple-element.20), channel_id=1, source_target_pairs={{1,0},{2,1},{3,2},{4,3},{5,4},{6,5},{7,6},{8,7},{9,8},{10,9},{11,1... | collective-permute-start | bytes 1572872 | tf_op jit(solution)/shard_map/ppermute | solution.py:429
  53.6 0.0 all-to-all-done.2.chip_ref
  53.6 0.2 shard_map.87
  53.9 1.0 %collective-permute-start.3 = (bf16[16,128,128]{2,1,0:T(8,128)(2,1)S(1)}, bf16[16,128,128]{2,1,0:T(8,128)(2,1)S(1)}, u32[]{:S(2)}, u32[]{:S(2)}) collective-permute-start(bf16[16,128,128]{2,1,0:T(8,128)(2,1)S(1)} %get-tuple-element.25), channel_id=1, source_target_pairs={{0,1},{1,0},{2,3},{3,2},{4,5},{5,4},{6,7},{7,6},{8,9},{9,8},{10,11... | collective-permute-start | bytes 1572872 | tf_op jit(solution)/shard_map/ppermute | solution.py:433
  54.9 13.4 %collective-permute-done.1.refs_2_ = bf16[128,2048]{1,0:T(8,128)(2,1)S(1)} collective-permute-done((bf16[128,2048]{1,0:T(8,128)(2,1)}, bf16[128,2048]{1,0:T(8,128)(2,1)S(1)}, u32[]{:S(2)}, u32[]{:S(2)}) %collective-permute-start.1) | collective-permute-done | bytes 524320 | tf_op jit(solution)/shard_map/ppermute | solution.py:429
  68.4 1.6 %copy-done = bf16[4,128,2048]{2,1,0:T(8,128)(2,1)S(1)} copy-done((bf16[4,128,2048]{2,1,0:T(8,128)(2,1)S(1)}, bf16[4,128,2048]{2,1,0:T(8,128)(2,1)}, u32[]{:S(2)}) %copy-start) | copy-done | bytes 2097176
  70.0 1.6 %copy-done.2 = bf16[4,128,2048]{2,1,0:T(8,128)(2,1)S(1)} copy-done((bf16[4,128,2048]{2,1,0:T(8,128)(2,1)S(1)}, bf16[4,128,2048]{2,1,0:T(8,128)(2,1)}, u32[]{:S(2)}) %copy-start.2) | copy-done | bytes 2097176
  71.6 1.9 %finish.2 = (bf16[128,2048]{1,0:T(8,128)(2,1)}, bf16[128,2048]{1,0:T(8,128)(2,1)}, bf16[128,2048]{1,0:T(8,128)(2,1)}, bf16[128,2048]{1,0:T(8,128)(2,1)}) custom-call(s32[1]{0:T(128)} %bitcast.refs_0_.c_ref, bf16[4,128,2048]{2,1,0:T(8,128)(2,1)S(1)} %copy-done.2, bf16[128,2048]{1,0:T(8,128)(2,1)S(1)} %collective-permute-done.1.refs_2_, ...), custom_call_target="tpu_custom_call" | custom-call | flops 300000000 | bytes 5000000 | tf_op jit(solution)/shard_map/finish/pallas_call | solution.py:397
  73.5 1.9 %finish.3 = (bf16[128,2048]{1,0:T(8,128)(2,1)}, bf16[128,2048]{1,0:T(8,128)(2,1)}, bf16[128,2048]{1,0:T(8,128)(2,1)}, bf16[128,2048]{1,0:T(8,128)(2,1)}) custom-call(s32[1]{0:T(128)S(6)} %sub.3.refs_0_, bf16[4,128,2048]{2,1,0:T(8,128)(2,1)S(1)} %copy-done.2, ...), custom_call_target="tpu_custom_call", output_to_operand_aliasing={{0}: (6, {}), {1}: (7, {}), {2}: (8, {}), {3}: (9, {})} | custom-call | flops 300000000 | bytes 5000000 | tf_op jit(solution)/shard_map/finish/pallas_call | solution.py:397
  (5 shorter events, 0.0 us)
Async XLA Ops:
  2.5 2.3 %collective-permute-start.2 = (bf16[16,144,128]{2,1,0:T(8,128)(2,1)S(1)}, bf16[16,144,128]{2,1,0:T(8,128)(2,1)S(1)}, u32[]{:S(2)}, u32[]{:S(2)}) collective-permute-start(bf16[16,144,128]{2,1,0:T(8,128)(2,1)S(1)} %get-tuple-element.22), channel_id=1, source_target_pairs={{0,1},{1,0},{2,3},{3,2},{4,5},{5,4},{6,7},{7,6},{8,9},{9,8},{10,11... | collective-permute-start | bytes 1769480 | tf_op jit(solution)/shard_map/ppermute | solution.py:421
  5.9 13.6 %all-to-all-start = ((bf16[16,144,128]{2,1,0:T(8,128)(2,1)}), bf16[16,144,128]{2,1,0:T(8,128)(2,1)S(1)}, u32[]{:S(2)}, u32[]{:S(2)}) async-start(bf16[16,144,128]{2,1,0:T(8,128)(2,1)} %get-tuple-element.23), calls=%async_computation | async-start | bytes 1179648 | tf_op jit(solution)/shard_map/all_to_all | solution.py:425
  20.3 17.7 %all-to-all-start.1 = ((bf16[8,80,128]{2,1,0:T(8,128)(2,1)}), bf16[8,80,128]{2,1,0:T(8,128)(2,1)S(1)}, u32[]{:S(2)}, u32[]{:S(2)}) async-start(bf16[8,80,128]{2,1,0:T(8,128)(2,1)} %shard_map.85), calls=%async_computation.1 | async-start | bytes 327680 | tf_op jit(solution)/shard_map/all_to_all | solution.py:428
  27.4 17.7 %collective-permute-start = (bf16[128,2048]{1,0:T(8,128)(2,1)S(1)}, bf16[128,2048]{1,0:T(8,128)(2,1)S(1)}, u32[]{:S(2)}, u32[]{:S(2)}) collective-permute-start(bf16[128,2048]{1,0:T(8,128)(2,1)S(1)} %get-tuple-element.18), channel_id=1, source_target_pairs={{0,1},{1,2},{2,3},{3,4},{4,5},{5,6},{6,7},{7,8},{8,9},{9,10},{10,1... | collective-permute-start | bytes 1572872 | tf_op jit(solution)/shard_map/ppermute | solution.py:422
  39.1 14.6 %all-to-all-start.2 = ((bf16[16,128,128]{2,1,0:T(8,128)(2,1)}), bf16[16,128,128]{2,1,0:T(8,128)(2,1)S(1)}, u32[]{:S(2)}, u32[]{:S(2)}) async-start(bf16[16,128,128]{2,1,0:T(8,128)(2,1)} %shard_map.86), calls=%async_computation.2 | async-start | bytes 1048576 | tf_op jit(solution)/shard_map/all_to_all | solution.py:431
  51.7 16.7 %collective-permute-start.1 = (bf16[128,2048]{1,0:T(8,128)(2,1)}, bf16[128,2048]{1,0:T(8,128)(2,1)S(1)}, u32[]{:S(2)}, u32[]{:S(2)}) collective-permute-start(bf16[128,2048]{1,0:T(8,128)(2,1)} %get-tuple-element.20), channel_id=1, source_target_pairs={{1,0},{2,1},{3,2},{4,3},{5,4},{6,5},{7,6},{8,7},{9,8},{10,9},{11,1... | collective-permute-start | bytes 1572872 | tf_op jit(solution)/shard_map/ppermute | solution.py:429
  53.9 19.6 %collective-permute-start.3 = (bf16[16,128,128]{2,1,0:T(8,128)(2,1)S(1)}, bf16[16,128,128]{2,1,0:T(8,128)(2,1)S(1)}, u32[]{:S(2)}, u32[]{:S(2)}) collective-permute-start(bf16[16,128,128]{2,1,0:T(8,128)(2,1)S(1)} %get-tuple-element.25), channel_id=1, source_target_pairs={{0,1},{1,0},{2,3},{3,2},{4,5},{5,4},{6,7},{7,6},{8,9},{9,8},{10,11... | collective-permute-start | bytes 1572872 | tf_op jit(solution)/shard_map/ppermute | solution.py:433
  68.4 1.6 %copy-start = (bf16[4,128,2048]{2,1,0:T(8,128)(2,1)S(1)}, bf16[4,128,2048]{2,1,0:T(8,128)(2,1)}, u32[]{:S(2)}) copy-start(bf16[4,128,2048]{2,1,0:T(8,128)(2,1)} %get-tuple-element.26.refs_5_) | copy-start | bytes 6291460
  70.0 1.6 %copy-start.2 = (bf16[4,128,2048]{2,1,0:T(8,128)(2,1)S(1)}, bf16[4,128,2048]{2,1,0:T(8,128)(2,1)}, u32[]{:S(2)}) copy-start(bf16[4,128,2048]{2,1,0:T(8,128)(2,1)} %get-tuple-element.19.refs_1_) | copy-start | bytes 6291460
  71.6 1.9 %copy-start.1 = (bf16[4,128,2048]{2,1,0:T(8,128)(2,1)S(1)}, bf16[4,128,2048]{2,1,0:T(8,128)(2,1)}, u32[]{:S(2)}) copy-start(bf16[4,128,2048]{2,1,0:T(8,128)(2,1)} %get-tuple-element.26.refs_5_) | copy-start | bytes 6291460
